TPU v7x, 32 devices: a whole 2x2x4 slice. The times are simulated.
32 devices in a mesh: groups: 2 (over y), strip: 8 (over z, x), chan: 2 (over core).
Axes of the slice: x: 2, y: 2, z: 4, core: 2. Of those that a mesh axis runs over, the one named last changes fastest.
Arguments:
- sky_cube: bfloat16 [32, 512, 1024], P('chan', 'strip', 'groups'), parts along dimension 2, may hold values from -80 to 80
- chan_flags: int32 [32], P('chan'), may hold values 0 or 1
Outputs:
- snr_peak: bfloat16 [32, 512, 1024], P('chan', 'strip', 'groups'), parts along dimension 2
There are 2 independent parts, one for each index of `groups`. A program takes and returns all parts, laid end to end along the dimension named above; an argument that names none is the same for every part. Nothing has to cross between parts.
All inputs are finite; a program needn't handle non-finite values. No bound on the sum of `chan_flags` on one device may be relied on, other than what follows from the above.
Results may differ from a plain program's by a relative error of at most 0.0054.
Values may be sent and summed in bfloat16 or wider, within the bound.
No kernel may reach another device: no remote copies, remote signals or barrier semaphores. Data moves between devices by JAX's collectives and lax.ppermute only.
A program may use at most 64 MiB of HBM per device.

v0:
```python
import math

import jax
import jax.numpy as jnp
import numpy as np
from jax import lax
from jax.sharding import PartitionSpec as P

boxcar_widths = (3, 7)
gauss_settings = ((5.0, 8), (10.0, 15))
epsilon = 1e-06
clip_level = 3.0


def extended(value, sides, width):
    for axis, dim in sides:
        devices, length = (lax.axis_size(axis), value.shape[dim])
        up = [(i, (i + 1) % devices) for i in range(devices - 1)]
        down = [(j, i) for i, j in up]
        last = lax.slice_in_dim(value, length - width, length, axis=dim)
        initial = lax.slice_in_dim(value, 0, width, axis=dim)
        before = lax.ppermute(last, axis, up)
        after = lax.ppermute(initial, axis, down)
        value = jnp.concatenate([before, value, after], axis=dim)
    return value


def gauss_weights(fwhm, radius):
    offsets = np.arange(-15, 16)
    spread = fwhm / (2.0 * math.sqrt(2.0 * math.log(2.0)))
    weights = np.exp(-(offsets**2) / (2.0 * spread**2)) * (np.abs(offsets) <= radius)
    weights = weights / weights.sum()
    return weights.astype(np.float32)


def column_matrix(weights):
    tap_index = np.arange(384)[:, None] - 128 - np.arange(128)[None, :] + 15
    inside = (tap_index >= 0) & (tap_index <= 30)
    matrix = np.where(inside, weights[np.clip(tap_index, 0, 30)], 0.0).astype(np.float32)
    return jnp.asarray(matrix).astype(jnp.bfloat16)


def row_matrix(weights, n_rows):
    tap_index = np.arange(n_rows + 30)[None, :] - np.arange(n_rows)[:, None]
    inside = (tap_index >= 0) & (tap_index <= 30)
    matrix = np.where(inside, weights[np.clip(tap_index, 0, 30)], 0.0).astype(np.float32)
    return jnp.asarray(matrix).astype(jnp.bfloat16)


def spectral_mean(padded, box_width, chan_count):
    half_width = box_width // 2
    running = jnp.zeros((chan_count,) + padded.shape[1:], jnp.float32)
    for offset in range(-half_width, half_width + 1):
        running = running + padded[3 + offset : 3 + offset + chan_count].astype(jnp.float32)
    return (running / box_width).astype(jnp.bfloat16)


def column_pass(values, matrix):
    chan_count, n_rows, n_cols = values.shape
    blocks = n_cols // 128
    shaped = values.reshape(chan_count, n_rows, blocks, 128)
    zero_block = jnp.zeros((chan_count, n_rows, 1, 128), jnp.bfloat16)
    padded = jnp.concatenate([zero_block, shaped, zero_block], axis=2)
    joined = jnp.concatenate([padded[:, :, :-2], padded[:, :, 1:-1], padded[:, :, 2:]], axis=3)
    result = jnp.dot(joined, matrix, preferred_element_type=jnp.float32)
    return result.reshape(chan_count, n_rows, n_cols)


def smooth_all(framed, n_rows):
    kernels = []
    for which in range(len(boxcar_widths)):
        framed_one = framed[which]
        kernels.append(framed_one[:, 15 : 15 + n_rows].astype(jnp.float32))
        for fwhm, radius in gauss_settings:
            weights = gauss_weights(fwhm, radius)
            row_band = row_matrix(weights, n_rows)
            rowwise = jnp.einsum(
                "or,crx->cox", row_band, framed_one, preferred_element_type=jnp.float32
            ).astype(jnp.bfloat16)
            kernels.append(column_pass(rowwise, column_matrix(weights)))
    return kernels


def shards(sky_cube, chan_flags):
    chan_count, n_rows, n_cols = sky_cube.shape
    keep_mask = (1 - chan_flags).astype(jnp.bfloat16)
    masked = sky_cube * keep_mask[:, None, None]
    widened = extended(masked, (("chan", 0),), 3)
    raw_framed = extended(widened, (("strip", 1),), 15)
    framed = jnp.stack(
        [spectral_mean(raw_framed, box_width, chan_count) for box_width in boxcar_widths]
    )
    pixels = n_rows * lax.axis_size("strip") * n_cols
    kernels = smooth_all(framed, n_rows)
    peak_ratio = None
    for smoothed in kernels:
        squares = smoothed * smoothed
        total_power = lax.psum(jnp.sum(squares, axis=(1, 2)), "strip")
        rough_sigma = jnp.sqrt(total_power / pixels + epsilon)
        clip_limit = (clip_level * rough_sigma) ** 2
        clipped = lax.psum(
            jnp.sum(jnp.minimum(squares, clip_limit[:, None, None]), axis=(1, 2)), "strip"
        )
        noise_sigma = jnp.sqrt(clipped / pixels + epsilon)
        ratio_now = smoothed / noise_sigma[:, None, None]
        peak_ratio = ratio_now if peak_ratio is None else jnp.maximum(peak_ratio, ratio_now)
    return (peak_ratio * keep_mask.astype(jnp.float32)[:, None, None]).astype(jnp.bfloat16)


def solution(mesh):
    in_specs = (P("chan", "strip", "groups"), P("chan"))
    out_specs = P("chan", "strip", "groups")
    return jax.shard_map(shards, mesh=mesh, in_specs=in_specs, out_specs=out_specs, check_vma=False)
```

profile of v0, /device:TPU:0, one launch (start us, length us, event | category | flops | bytes accessed | tf_op | source)
XLA Modules:
  0.0 95.3 jit_solution(14626965517978023406)
XLA Ops:
  0.0 0.7 fusion.51
  0.7 1.4 %broadcast_multiply_fusion = bf16[16,64,512]{2,1,0:T(8,128)(2,1)S(1)} fusion(bf16[16,64,512]{2,1,0:T(8,128)(2,1)} %param.10, bf16[16]{0:T(256)(128)(2,1)S(1)} %get-tuple-element.32), kind=kLoop, calls=%fused_computation.85 | loop fusion | flops 524288 | bytes 2097184 | tf_op jit(solution)/shard_map/mul | solution.py:87
  2.1 2.4 %collective-permute-start = (bf16[3,64,512]{2,1,0:T(8,128)(2,1)S(1)}, bf16[3,64,512]{2,1,0:T(8,128)(2,1)S(1)}, u32[]{:S(2)}, u32[]{:S(2)}) collective-permute-start(bf16[3,64,512]{2,1,0:T(8,128)(2,1)S(1)} %get-tuple-element.29), channel_id=1, source_target_pairs={{0,1},{2,3},{4,5},{6,7},{8,9},{10,11},{12,13},{14,15},{16,17},{18,... | collective-permute-start | bytes 589832 | tf_op jit(solution)/shard_map/ppermute | solution.py:22
  4.5 1.3 %collective-permute-start.1 = (bf16[3,64,512]{2,1,0:T(8,128)(2,1)S(1)}, bf16[3,64,512]{2,1,0:T(8,128)(2,1)S(1)}, u32[]{:S(2)}, u32[]{:S(2)}) collective-permute-start(bf16[3,64,512]{2,1,0:T(8,128)(2,1)S(1)} %get-tuple-element.30), channel_id=1, source_target_pairs={{1,0},{3,2},{5,4},{7,6},{9,8},{11,10},{13,12},{15,14},{17,16},{19,... | collective-permute-start | bytes 589832 | tf_op jit(solution)/shard_map/ppermute | solution.py:23
  5.8 0.0 collective-permute-done
  5.8 2.0 %collective-permute-done.1 = bf16[3,64,512]{2,1,0:T(8,128)(2,1)S(1)} collective-permute-done((bf16[3,64,512]{2,1,0:T(8,128)(2,1)S(1)}, bf16[3,64,512]{2,1,0:T(8,128)(2,1)S(1)}, u32[]{:S(2)}, u32[]{:S(2)}) %collective-permute-start.1) | collective-permute-done | bytes 196640 | tf_op jit(solution)/shard_map/ppermute | solution.py:23
  7.8 0.1 pad_maximum_fusion.3
  7.9 4.2 %collective-permute-start.2 = (bf16[22,15,512]{2,1,0:T(8,128)(2,1)S(1)}, bf16[22,15,512]{2,1,0:T(8,128)(2,1)S(1)}, u32[]{:S(2)}, u32[]{:S(2)}) collective-permute-start(bf16[22,15,512]{2,1,0:T(8,128)(2,1)S(1)} %get-tuple-element.19), channel_id=1, source_target_pairs={{0,2},{2,4},{4,6},{6,8},{8,10},{10,12},{12,14},{1,3},{3,5},{5,7},{... | collective-permute-start | bytes 1013768 | tf_op jit(solution)/shard_map/ppermute | solution.py:22
  12.2 1.3 %collective-permute-start.3 = (bf16[22,15,512]{2,1,0:T(8,128)(2,1)S(1)}, bf16[22,15,512]{2,1,0:T(8,128)(2,1)S(1)}, u32[]{:S(2)}, u32[]{:S(2)}) collective-permute-start(bf16[22,15,512]{2,1,0:T(8,128)(2,1)S(1)} %get-tuple-element.20), channel_id=1, source_target_pairs={{2,0},{4,2},{6,4},{8,6},{10,8},{12,10},{14,12},{3,1},{5,3},{7,5},{... | collective-permute-start | bytes 1013768 | tf_op jit(solution)/shard_map/ppermute | solution.py:23
  13.5 14.4 %collective-permute-done.2 = bf16[22,15,512]{2,1,0:T(8,128)(2,1)S(1)} collective-permute-done((bf16[22,15,512]{2,1,0:T(8,128)(2,1)S(1)}, bf16[22,15,512]{2,1,0:T(8,128)(2,1)S(1)}, u32[]{:S(2)}, u32[]{:S(2)}) %collective-permute-start.2) | collective-permute-done | bytes 337952 | tf_op jit(solution)/shard_map/ppermute | solution.py:22
  27.8 0.0 collective-permute-done.3
  27.8 1.2 %pad_maximum_fusion = bf16[22,94,512]{2,1,0:T(8,128)(2,1)S(1)} fusion(bf16[22,15,512]{2,1,0:T(8,128)(2,1)S(1)} %collective-permute-done.3, bf16[3,64,512]{2,1,0:T(8,128)(2,1)S(1)} %collective-permute-done.1, bf16[16,64,512]{2,1,0:T(8,128)(2,1)S(1)} %broadcast_multiply_fusion, bf16[3,64,512]{2,1,0:T(8,128)(2,1)S(1)} %collective-permute-done, ...), kind=kLoop, calls=%fused_computation.43 | loop fusion | flops 10588160 | bytes 4235264 | tf_op jit(solution)/shard_map/concatenate | solution.py:24
  29.0 0.0 copy-start.4
  29.0 2.1 %fusion.1 = (bf16[16,94,512]{2,1,0:T(8,128)(2,1)S(1)}, bf16[16,94,512]{2,1,0:T(8,128)(2,1)S(1)}) fusion(bf16[22,94,512]{2,1,0:T(8,128)(2,1)S(1)} %pad_maximum_fusion), kind=kLoop, calls=%fused_computation.6 | loop fusion | flops 14630912 | bytes 13860864 | tf_op jit(solution)/shard_map/convert_element_type | solution.py:55
  31.2 0.0 copy-start.5
  31.2 0.4 fusion.43
  31.6 0.3 copy-done.5
  31.9 0.4 fusion.44
  32.3 0.4 fusion.45
  32.8 0.4 fusion.46
  33.2 0.8 fusion.31
  34.0 0.3 copy.68
  34.3 0.5 pad_slice_fusion.7
  34.8 0.3 copy.67
  35.1 0.5 pad_slice_fusion.5
  35.5 0.3 copy.66
  35.8 0.5 pad_slice_fusion.3
  36.3 0.3 copy.65
  36.6 0.0 copy-start.7
  36.6 0.5 pad_slice_fusion.1
  37.1 0.4 copy-done.7
  37.5 2.4 %multiply_reduce_fusion.3 = (f32[16]{0:T(128)S(1)}, f32[16,64,4,128]{3,1,2,0:T(8,128)}) fusion(bf16[384,128,1,1]{1,0,3,2:T(8,128)(2,1)S(1)} %copy-done.7, bf16[16,64,4,128]{3,1,2,0:T(8,128)(2,1)S(1)} %get-tuple-element.22, bf16[16,64,4,128]{3,1,2,0:T(8,128)(2,1)S(1)} %bitcast.85, bf16[16,64,4,128]{3,1,2,0:T(8,128)(2,1)S(1)} %get-tuple-element.21), kind=kOutput, calls=%fused_computation.64 | convolution fusion | flops 413138944 | bytes 5341248 | tf_op jit(solution)/shard_map/dot_general | solution.py:65
  39.8 2.3 %multiply_reduce_fusion.1 = (f32[16]{0:T(128)S(1)}, f32[16,64,4,128]{3,1,2,0:T(8,128)}) fusion(bf16[384,128,1,1]{1,0,3,2:T(8,128)(2,1)S(1)} %copy-done.7, bf16[16,64,4,128]{3,1,2,0:T(8,128)(2,1)S(1)} %get-tuple-element.26, bf16[16,64,4,128]{3,1,2,0:T(8,128)(2,1)S(1)} %bitcast.87, bf16[16,64,4,128]{3,1,2,0:T(8,128)(2,1)S(1)} %get-tuple-element.25), kind=kOutput, calls=%fused_computation.62 | convolution fusion | flops 413138944 | bytes 5341248 | tf_op jit(solution)/shard_map/dot_general | solution.py:65
  42.1 2.3 %multiply_reduce_fusion.2 = (f32[16]{0:T(128)S(1)}, f32[16,64,4,128]{3,1,2,0:T(8,128)}) fusion(bf16[384,128,1,1]{1,0,3,2:T(8,128)(2,1)S(1)} %copy-done.6, bf16[16,64,4,128]{3,1,2,0:T(8,128)(2,1)S(1)} %get-tuple-element.24, bf16[16,64,4,128]{3,1,2,0:T(8,128)(2,1)S(1)} %bitcast.81, bf16[16,64,4,128]{3,1,2,0:T(8,128)(2,1)S(1)} %get-tuple-element.23), kind=kOutput, calls=%fused_computation.63 | convolution fusion | flops 413138944 | bytes 5341248 | tf_op jit(solution)/shard_map/dot_general | solution.py:65
  44.5 2.3 %multiply_reduce_fusion = (f32[16]{0:T(128)S(1)}, f32[16,64,4,128]{3,1,2,0:T(8,128)}) fusion(bf16[384,128,1,1]{1,0,3,2:T(8,128)(2,1)S(1)} %copy-done.6, bf16[16,64,4,128]{3,1,2,0:T(8,128)(2,1)S(1)} %get-tuple-element.28, bf16[16,64,4,128]{3,1,2,0:T(8,128)(2,1)S(1)} %bitcast.83, bf16[16,64,4,128]{3,1,2,0:T(8,128)(2,1)S(1)} %get-tuple-element.27), kind=kOutput, calls=%fused_computation.61 | convolution fusion | flops 413138944 | bytes 5341248 | tf_op jit(solution)/shard_map/dot_general | solution.py:65
  46.8 21.8 %all-reduce.9 = (f32[16]{0:T(128)S(1)}, f32[16]{0:T(128)S(1)}, f32[16]{0:T(128)S(1)}, f32[16]{0:T(128)S(1)}, f32[16]{0:T(128)S(1)}, /*index=5*/f32[16]{0:T(128)S(1)}) all-reduce(f32[16]{0:T(128)S(1)} %get-tuple-element.33, f32[16]{0:T(128)S(1)} %get-tuple-element.35, ...), channel_id=1, replica_groups=mesh['groups'=2,'strip'=8,'chan'=2] {'strip'}, use_global_device_ids=true, to_apply=%region_21.0 | all-reduce | flops 96 | bytes 768 | tf_op jit(solution)/shard_map/psum | solution.py:98
  68.6 0.6 fusion.35
  69.2 0.6 fusion.34
  69.8 0.4 copy-done
  70.2 0.4 minimum_reduce_fusion.3
  70.5 0.2 copy-done.2
  70.8 0.4 minimum_reduce_fusion.2
  71.2 0.7 copy-done.1
  71.9 0.4 minimum_reduce_fusion.1
  72.3 0.2 copy-done.3
  72.5 0.4 minimum_reduce_fusion
  72.9 17.1 %all-reduce.8 = (f32[16]{0:T(128)S(1)}, f32[16]{0:T(128)S(1)}, f32[16]{0:T(128)S(1)}, f32[16]{0:T(128)S(1)}, f32[16]{0:T(128)S(1)}, /*index=5*/f32[16]{0:T(128)S(1)}) all-reduce(f32[16]{0:T(128)S(1)} %minimum_reduce_fusion, f32[16]{0:T(128)S(1)} %minimum_reduce_fusion.1, ...), channel_id=1, replica_groups=mesh['groups'=2,'strip'=8,'chan'=2] {'strip'}, use_global_device_ids=true, to_apply=%region_23.0 | all-reduce | flops 96 | bytes 768 | tf_op jit(solution)/shard_map/psum | solution.py:101
  90.1 5.2 %fusion.42 = bf16[16,64,512]{2,1,0:T(8,128)(2,1)} fusion(f32[16]{0:T(128)S(1)} %get-tuple-element.31, f32[16]{0:T(128)S(1)} %add_sqrt_fusion, f32[16]{0:T(128)S(1)} %add_sqrt_fusion.1, f32[16]{0:T(128)S(1)} %add_sqrt_fusion.2, f32[16]{0:T(128)S(1)} %add_sqrt_fusion.3, f32[16]{0:T(128)S(1)} %add_sqrt_fusion.4, f32[16]{0:T(128)S(1)} %add_sqrt_fusion.5, ...), kind=kLoop, calls=%fused_computation.60 | loop fusion | flops 7864320 | bytes 11534784 | tf_op jit(solution)/shard_map/convert_element_type | solution.py:107
  (20 shorter events, 0.1 us)
Async XLA Ops:
  2.1 3.7 %collective-permute-start = (bf16[3,64,512]{2,1,0:T(8,128)(2,1)S(1)}, bf16[3,64,512]{2,1,0:T(8,128)(2,1)S(1)}, u32[]{:S(2)}, u32[]{:S(2)}) collective-permute-start(bf16[3,64,512]{2,1,0:T(8,128)(2,1)S(1)} %get-tuple-element.29), channel_id=1, source_target_pairs={{0,1},{2,3},{4,5},{6,7},{8,9},{10,11},{12,13},{14,15},{16,17},{18,... | collective-permute-start | bytes 589832 | tf_op jit(solution)/shard_map/ppermute | solution.py:22
  4.5 3.3 %collective-permute-start.1 = (bf16[3,64,512]{2,1,0:T(8,128)(2,1)S(1)}, bf16[3,64,512]{2,1,0:T(8,128)(2,1)S(1)}, u32[]{:S(2)}, u32[]{:S(2)}) collective-permute-start(bf16[3,64,512]{2,1,0:T(8,128)(2,1)S(1)} %get-tuple-element.30), channel_id=1, source_target_pairs={{1,0},{3,2},{5,4},{7,6},{9,8},{11,10},{13,12},{15,14},{17,16},{19,... | collective-permute-start | bytes 589832 | tf_op jit(solution)/shard_map/ppermute | solution.py:23
  7.9 19.9 %collective-permute-start.2 = (bf16[22,15,512]{2,1,0:T(8,128)(2,1)S(1)}, bf16[22,15,512]{2,1,0:T(8,128)(2,1)S(1)}, u32[]{:S(2)}, u32[]{:S(2)}) collective-permute-start(bf16[22,15,512]{2,1,0:T(8,128)(2,1)S(1)} %get-tuple-element.19), channel_id=1, source_target_pairs={{0,2},{2,4},{4,6},{6,8},{8,10},{10,12},{12,14},{1,3},{3,5},{5,7},{... | collective-permute-start | bytes 1013768 | tf_op jit(solution)/shard_map/ppermute | solution.py:22
  12.2 15.7 %collective-permute-start.3 = (bf16[22,15,512]{2,1,0:T(8,128)(2,1)S(1)}, bf16[22,15,512]{2,1,0:T(8,128)(2,1)S(1)}, u32[]{:S(2)}, u32[]{:S(2)}) collective-permute-start(bf16[22,15,512]{2,1,0:T(8,128)(2,1)S(1)} %get-tuple-element.20), channel_id=1, source_target_pairs={{2,0},{4,2},{6,4},{8,6},{10,8},{12,10},{14,12},{3,1},{5,3},{7,5},{... | collective-permute-start | bytes 1013768 | tf_op jit(solution)/shard_map/ppermute | solution.py:23
  29.0 2.1 %copy-start.4 = (bf16[64,94,1]{1,0,2:T(8,128)(2,1)S(1)}, bf16[64,94,1]{1,0,2:T(8,128)(2,1)}, u32[]{:S(2)}) copy-start(bf16[64,94,1]{1,0,2:T(8,128)(2,1)} %constant.62) | copy-start | bytes 36100
  31.2 0.7 copy-start.5
  36.6 0.9 copy-start.7
  39.8 2.3 %copy-start.6 = (bf16[384,128,1,1]{1,0,3,2:T(8,128)(2,1)S(1)}, bf16[384,128,1,1]{1,0,3,2:T(8,128)(2,1)}, u32[]{:S(2)}) copy-start(bf16[384,128,1,1]{1,0,3,2:T(8,128)(2,1)} %constant.65) | copy-start | bytes 294916
  68.6 1.6 %copy-start = (f32[16,64,4,128]{3,1,2,0:T(8,128)S(1)}, f32[16,64,4,128]{3,1,2,0:T(8,128)}, u32[]{:S(2)}) copy-start(f32[16,64,4,128]{3,1,2,0:T(8,128)} %get-tuple-element.40) | copy-start | bytes 6291460
  68.6 2.2 %copy-start.2 = (f32[16,64,4,128]{3,1,2,0:T(8,128)S(1)}, f32[16,64,4,128]{3,1,2,0:T(8,128)}, u32[]{:S(2)}) copy-start(f32[16,64,4,128]{3,1,2,0:T(8,128)} %get-tuple-element.38) | copy-start | bytes 6291460
  70.2 1.7 %copy-start.1 = (f32[16,64,4,128]{3,1,2,0:T(8,128)S(1)}, f32[16,64,4,128]{3,1,2,0:T(8,128)}, u32[]{:S(2)}) copy-start(f32[16,64,4,128]{3,1,2,0:T(8,128)} %get-tuple-element.36) | copy-start | bytes 6291460
  70.8 1.7 %copy-start.3 = (f32[16,64,4,128]{3,1,2,0:T(8,128)S(1)}, f32[16,64,4,128]{3,1,2,0:T(8,128)}, u32[]{:S(2)}) copy-start(f32[16,64,4,128]{3,1,2,0:T(8,128)} %get-tuple-element.34) | copy-start | bytes 6291460
where the time goes:
time: 95.6 us; the launch traced here: 95.3 us
  blocking collectives  38.9 us (41%)
  waiting for transfers between devices  16.4 us (17%)
  other arithmetic  14.2 us (15%)
  matrix products  11 us (12%)
  starting transfers between devices  9.23 us (10%)
  local copies, waits for them, and re-layouts  5.26 us (6%)
    psum x1, blocking collectives, shards(): total_power = lax.psum(jnp.sum(squares, axis=(1, 2)), 'strip')  21.8 us
    psum x1, blocking collectives, shards(): lax.psum(jnp.sum(jnp.minimum(squares, clip_limit[:, None, None]), axis=(1...  17.1 us
    ppermute x2, waiting for transfers between devices, extended(): before = lax.ppermute(last, axis, up)  14.4 us
    dot_general x4, matrix products, column_pass(): result = jnp.dot(joined, matrix, preferred_element_type=jnp.float32)  9.33 us
    ppermute x2, starting transfers between devices, extended(): before = lax.ppermute(last, axis, up)  6.64 us
    convert_element_type x1, other arithmetic, shards(): (peak_ratio * keep_mask.astype(jnp.float32)[:, None, None]).astype(jnp.bf...  5.19 us
    reduce_sum x6, other arithmetic, shards(): jnp.sum(jnp.minimum(squares, clip_limit[:, None, None]), axis=(1, 2))  2.66 us
    ppermute x2, starting transfers between devices, extended(): after = lax.ppermute(initial, axis, down)  2.58 us
  transfers between devices with their start and end apart: 4, of which 2 were waited for; matrix products, arithmetic and copies ran while one was open for 0% of the time, Pallas kernels for 0%

commit v1 on v0

v1 whole, which is shorter than its diff:
```python
import functools
import math

import jax
import jax.numpy as jnp
import numpy as np
from jax import lax
from jax.experimental import pallas as pl
from jax.experimental.pallas import tpu as pltpu
from jax.sharding import PartitionSpec as P

boxcar_widths = (3, 7)
gauss_settings = ((5.0, 8), (10.0, 15))
epsilon = 1e-06
clip_level = 3.0
RIM = 3
REACH = 15
EDGE = 16
LANES = 128
VMEM = pltpu.VMEM
SMEM = pltpu.SMEM


def gauss_weights(fwhm, radius):
    offsets = np.arange(-REACH, REACH + 1)
    spread = fwhm / (2.0 * math.sqrt(2.0 * math.log(2.0)))
    weights = np.exp(-(offsets**2) / (2.0 * spread**2)) * (np.abs(offsets) <= radius)
    weights = weights / weights.sum()
    return weights.astype(np.float32)


def band(out_positions, in_positions):
    offset = np.asarray(in_positions)[None, :] - np.asarray(out_positions)[:, None]
    inside = np.abs(offset) <= REACH
    index = np.clip(offset + REACH, 0, 2 * REACH)
    return np.stack([np.where(inside, gauss_weights(*s)[index], 0.0) for s in gauss_settings])


def constant(matrix):
    return jnp.asarray(matrix.astype(np.float32)).astype(jnp.bfloat16)


def square_sum(values):
    rows, cols = values.shape
    return fold(values * values)


def fold(values):
    rows, cols = values.shape
    total = None
    for r in range(0, rows, 8):
        for c in range(0, cols, LANES):
            part = values[r : r + 8, c : c + LANES]
            total = part if total is None else total + part
    return total


def spectral_tiles(load, store, chan_count):
    x = [load(c) for c in range(-RIM, chan_count + RIM)]
    for c in range(chan_count):
        s3 = x[c + 2] + x[c + 3] + x[c + 4]
        s7 = (x[c] + x[c + 1]) + s3 + (x[c + 5] + x[c + 6])
        store(0, c, (s3 * (1.0 / 3.0)).astype(jnp.bfloat16))
        store(1, c, (s7 * (1.0 / 7.0)).astype(jnp.bfloat16))


def column_pass(rows_ref, matrix_ref, out_ref, acc_ref, chan_count, block):
    per = rows_ref.shape[1] // (2 * chan_count)
    step = per * block
    for f in range(2):

        @pl.loop(0, 2 * chan_count // block)
        def _(m):
            start = pl.multiple_of(m * step, step)
            result = jnp.dot(
                rows_ref[f, pl.ds(start, step), :], matrix_ref[f], preferred_element_type=jnp.float32
            )
            out_ref[f, pl.ds(start, step), :] = result
            for i in range(block):
                slot = m * block + i
                k = lax.div(slot, chan_count) * 3 + 1 + f
                acc_ref[k * chan_count + lax.rem(slot, chan_count)] = square_sum(
                    result[i * per : (i + 1) * per]
                )


def middle_kernel(flags, sides, sky, rim, row_band, col_band, spec, smooth, sums, rowwise, acc):
    chan_count, n_rows, n_cols = sky.shape
    keep = [(1 - flags[c]).astype(jnp.float32) for c in range(chan_count)]
    side = [sides[i].astype(jnp.float32) for i in range(2)]

    @pl.loop(0, n_rows // 16)
    def _(t):
        rows = pl.ds(pl.multiple_of(t * 16, 16), 16)
        for lane in range(0, n_cols, LANES):
            cols = slice(lane, lane + LANES)

            def load(c):
                if c < 0:
                    return rim[0, c + RIM, rows, cols].astype(jnp.float32) * side[0]
                if c >= chan_count:
                    return rim[rim.shape[0] - 1, c - chan_count, rows, cols].astype(jnp.float32) * side[1]
                return sky[c, rows, cols].astype(jnp.float32) * keep[c]

            def store(w, c, value):
                spec[w, c, rows, cols] = value

            spectral_tiles(load, store, chan_count)

    per = rowwise.shape[1] // (2 * chan_count)

    @pl.loop(0, chan_count)
    def _(c):
        for w in range(2):
            plane = spec[w, c]
            acc[w * 3 * chan_count + c] = square_sum(plane.astype(jnp.float32))
            row = jnp.dot(row_band[...], plane, preferred_element_type=jnp.float32).astype(jnp.bfloat16)
            start = pl.multiple_of((w * chan_count + c) * per, per)
            for f in range(2):
                rowwise[f, pl.ds(start, per), :] = row[f * per : (f + 1) * per]

    column_pass(rowwise, col_band, smooth, acc, chan_count, 4)
    sums[...] = jnp.sum(acc[...], axis=1)


def share(acc_sum, peers):
    rows = acc_sum.shape[0]
    if rows < LANES:
        acc_sum = jnp.concatenate([acc_sum, jnp.zeros((LANES - rows, LANES), jnp.float32)], axis=0)
    total = jnp.sum(acc_sum.T, axis=0, keepdims=True)
    return jnp.broadcast_to(total, (peers, LANES))


def spread(shared):
    total = jnp.sum(shared, axis=0, keepdims=True)
    return jnp.broadcast_to(total, (LANES, LANES)).T


def edge_kernel(
    flags, sides, above, below, corner_above, corner_below, spec, row_band, col_band, sums, smooth, shared, rowwise, acc, frame
):
    chan_count, edge, n_cols = above.shape
    n_rows = spec.shape[2]
    keep = [(1 - flags[c]).astype(jnp.float32) for c in range(chan_count)]
    side = [sides[i].astype(jnp.float32) for i in range(2)]
    for strip, corner, base in ((above, corner_above, 0), (below, corner_below, edge + n_rows)):
        for lane in range(0, n_cols, LANES):
            cols = slice(lane, lane + LANES)

            def load(c):
                if c < 0:
                    return corner[0, c + RIM, :, cols].astype(jnp.float32) * side[0]
                if c >= chan_count:
                    return corner[corner.shape[0] - 1, c - chan_count, :, cols].astype(jnp.float32) * side[1]
                return strip[c, :, cols].astype(jnp.float32) * keep[c]

            def store(w, c, value):
                frame[w, c, base : base + edge, cols] = value

            spectral_tiles(load, store, chan_count)
    frame[:, :, edge : edge + n_rows, :] = spec[...]
    per = rowwise.shape[1] // (2 * chan_count)

    @pl.loop(0, chan_count)
    def _(c):
        for w in range(2):
            row = jnp.dot(row_band[...], frame[w, c], preferred_element_type=jnp.float32).astype(jnp.bfloat16)
            start = pl.multiple_of((w * chan_count + c) * per, per)
            for f in range(2):
                rowwise[f, pl.ds(start, per), :] = row[f * per : (f + 1) * per]

    acc[...] = jnp.zeros_like(acc)
    column_pass(rowwise, col_band, smooth, acc, chan_count, 4)
    shared[...] = share(sums[...] + jnp.sum(acc[...], axis=1), shared.shape[0])


def clip_kernel(pixels, shared_in, spec, middle, edges, shared, limit, acc):
    chan_count = spec.shape[1]
    rough = jnp.sqrt(spread(shared_in[...]) / pixels + epsilon)
    limit[...] = (clip_level * rough) ** 2
    per = middle.shape[1] // (2 * chan_count)

    @pl.loop(0, chan_count)
    def _(c):
        for w in range(2):
            start = pl.multiple_of((w * chan_count + c) * per, per)
            for f in range(-1, 2):
                slot = (w * 3 + 1 + f) * chan_count + c
                top = jnp.broadcast_to(limit[pl.ds(slot, 1), :], (8, LANES))
                total = None
                if f < 0:
                    parts = [spec[w, c].astype(jnp.float32)]
                else:
                    parts = [middle[f, pl.ds(start, per), :], edges[f, pl.ds(start, per), :]]
                for part in parts:
                    for r in range(0, part.shape[0], 8):
                        for l in range(0, part.shape[1], LANES):
                            value = part[r : r + 8, l : l + LANES]
                            value = jnp.minimum(value * value, top)
                            total = value if total is None else total + value
                acc[slot] = total

    shared[...] = share(jnp.sum(acc[...], axis=1), shared.shape[0])


def ratio_kernel(pixels, flags, shared_in, spec, middle, edges, out, scale):
    chan_count, n_rows, n_cols = out.shape
    edge = EDGE
    scale[...] = 1.0 / jnp.sqrt(spread(shared_in[...]) / pixels + epsilon)
    per = middle.shape[1] // (2 * chan_count)

    @pl.loop(0, chan_count)
    def _(c):
        keep = (1 - flags[c]).astype(jnp.float32)
        factors = [
            jnp.broadcast_to(scale[pl.ds(k * chan_count + c, 1), :], (16, LANES)) for k in range(6)
        ]
        for r in range(0, n_rows, 16):
            if r < edge:
                source, offset = edges, r
            elif r < n_rows - edge:
                source, offset = middle, r - edge
            else:
                source, offset = edges, r - (n_rows - edge) + edge
            for l in range(0, n_cols, LANES):
                cols = slice(l, l + LANES)
                best = None
                for w in range(2):
                    values = [spec[w, c, r : r + 16, cols].astype(jnp.float32)]
                    start = pl.multiple_of((w * chan_count + c) * per, per) + offset
                    start = pl.multiple_of(start, 16)
                    values += [source[f, pl.ds(start, 16), cols] for f in range(2)]
                    for f in range(3):
                        value = values[f] * factors[w * 3 + f]
                        best = value if best is None else jnp.maximum(best, value)
                out[c, r : r + 16, cols] = (best * keep).astype(jnp.bfloat16)


def specs(*spaces):
    return [pl.BlockSpec(memory_space=s) for s in spaces]


def shards(sky_cube, chan_flags):
    chan_count, n_rows, n_cols = sky_cube.shape
    strips, blocks = lax.axis_size("strip"), lax.axis_size("chan")
    pixels = n_rows * strips * n_cols
    keep_mask = (1 - chan_flags).astype(jnp.bfloat16)
    block = lax.axis_index("chan")

    down = [(i, i + 1) for i in range(strips - 1)]
    up = [(j, i) for i, j in down]
    above = lax.ppermute(sky_cube[:, n_rows - EDGE :], "strip", down)
    below = lax.ppermute(sky_cube[:, :EDGE], "strip", up)

    last = sky_cube[chan_count - RIM :] * keep_mask[chan_count - RIM :, None, None]
    first = sky_cube[:RIM] * keep_mask[:RIM, None, None]
    forth = [(i, i + 1) for i in range(blocks - 1)]
    back = [(j, i) for i, j in forth]
    if blocks == 2:
        moves = [(jnp.where(block == 0, last, first), forth + back)]
    else:
        moves = [(last, forth), (first, back)]
    rim, corner_above, corner_below = [], [], []
    for payload, pairs in moves:
        rim.append(lax.ppermute(payload, "chan", pairs))
        for rows, strip_pairs, into in (
            (payload[:, n_rows - EDGE :], down, corner_above),
            (payload[:, :EDGE], up, corner_below),
        ):
            both = [(s * blocks + a, t * blocks + b) for s, t in strip_pairs for a, b in pairs]
            into.append(lax.ppermute(rows, ("strip", "chan"), both))
    rim, corner_above, corner_below = (jnp.stack(v) for v in (rim, corner_above, corner_below))
    sides = jnp.stack([block > 0, block < blocks - 1]).astype(jnp.int32)

    mid = n_rows - 2 * EDGE
    own = np.arange(n_rows)
    mid_band = constant(band(own[EDGE : n_rows - EDGE], own).reshape(2 * mid, n_rows))
    edge_rows = np.concatenate([own[:EDGE], own[n_rows - EDGE :]])
    framed = np.arange(-EDGE, n_rows + EDGE)
    edge_band = constant(band(edge_rows, framed).reshape(4 * EDGE, n_rows + 2 * EDGE))
    cols = np.arange(n_cols)
    col_band = constant(band(cols, cols).transpose(0, 2, 1))

    f32, bf16 = jnp.float32, jnp.bfloat16
    slots = 6 * chan_count
    params = pltpu.CompilerParams(vmem_limit_bytes=32 * 2**20)

    def call(kernel, ins, outs, scratch, flops, name):
        return pl.pallas_call(
            kernel,
            in_specs=specs(*ins),
            out_specs=specs(*[VMEM] * len(outs)),
            out_shape=[jax.ShapeDtypeStruct(s, d) for s, d in outs],
            scratch_shapes=[VMEM(s, d) for s, d in scratch],
            compiler_params=params,
            cost_estimate=pl.CostEstimate(flops=flops, bytes_accessed=8 * 2**20, transcendentals=0),
            name=name,
        )

    spec, middle, sums = call(
        middle_kernel,
        [SMEM, SMEM] + [VMEM] * 4,
        [
            ((2, chan_count, n_rows, n_cols), bf16),
            ((2, 2 * chan_count * mid, n_cols), f32),
            ((slots, LANES), f32),
        ],
        [((2, 2 * chan_count * mid, n_cols), bf16), ((slots, 8, LANES), f32)],
        2 * 10**9,
        "middle_rows",
    )(chan_flags, sides, sky_cube, rim, mid_band, col_band)
    edges, shared = call(
        edge_kernel,
        [SMEM, SMEM] + [VMEM] * 8,
        [((2, 4 * chan_count * EDGE, n_cols), f32), ((strips, LANES), f32)],
        [
            ((2, 4 * chan_count * EDGE, n_cols), bf16),
            ((slots, 8, LANES), f32),
            ((2, chan_count, n_rows + 2 * EDGE, n_cols), bf16),
        ],
        2 * 10**9,
        "edge_rows",
    )(chan_flags, sides, above, below, corner_above, corner_below, spec, edge_band, col_band, sums)
    shared = lax.all_to_all(shared, "strip", 0, 0, tiled=True)
    (shared,) = call(
        functools.partial(clip_kernel, pixels),
        [VMEM] * 4,
        [((strips, LANES), f32)],
        [((LANES, LANES), f32), ((slots, 8, LANES), f32)],
        10**8,
        "clip",
    )(shared, spec, middle, edges)
    shared = lax.all_to_all(shared, "strip", 0, 0, tiled=True)
    (out,) = call(
        functools.partial(ratio_kernel, pixels),
        [SMEM] + [VMEM] * 4,
        [((chan_count, n_rows, n_cols), bf16)],
        [((LANES, LANES), f32)],
        10**8,
        "ratio",
    )(chan_flags, shared, spec, middle, edges)
    return out


def solution(mesh):
    in_specs = (P("chan", "strip", "groups"), P("chan"))
    out_specs = P("chan", "strip", "groups")
    return jax.shard_map(shards, mesh=mesh, in_specs=in_specs, out_specs=out_specs, check_vma=False)
```

time: 95.6 us -> 62.8 us (0.66)
  Pallas kernels: 0 us -> 20.6 us
  blocking collectives: 38.9 us -> 21.4 us
  waiting for transfers between devices: 16.4 us -> 0.01 us
  other arithmetic: 14.2 us -> 1.85 us
  matrix products: 11 us -> 0 us
  starting transfers between devices: 9.23 us -> 13.4 us
    psum x2 -> x0, blocking collectives: 38.9 us -> none  [the longest x1 21.8 us: shards(): total_power = lax.psum(jnp.sum(squares, axis=(1, 2)), 'strip')]
    all_to_all x0 -> x2, blocking collectives: none -> 21.4 us  [shards(): shared = lax.all_to_all(shared, 'strip', 0, 0, tiled=True)]
    pallas_call x0 -> x4, Pallas kernels: none -> 20.6 us  [the longest x1 8.05 us: shards(): call(middle_kernel, [SMEM, SMEM] + [VMEM] * 4, [((2, chan_count, n_rows,...]
    ppermute x4 -> x5, waiting for transfers between devices: 16.4 us -> 0.01 us  [the longest x2 0.01 us: shards(): into.append(lax.ppermute(rows, ('strip', 'chan'), both))]
    dot_general x8 -> x0, matrix products: 11 us -> none  [the longest x4 9.33 us: column_pass(): result = jnp.dot(joined, matrix, preferred_element_type=jnp.float32)]
    convert_element_type x3 -> x2, other arithmetic: 7.96 us -> 0.73 us  [the longest x1 0.66 us: shards(): keep_mask = (1 - chan_flags).astype(jnp.bfloat16)]
    ppermute x4 -> x5, starting transfers between devices: 9.23 us -> 13.4 us  [the longest x2 6.41 us: shards(): into.append(lax.ppermute(rows, ('strip', 'chan'), both))]
    reduce_sum x7 -> x0, other arithmetic: 3.5 us -> none  [the longest x6 2.66 us: shards(): jnp.sum(jnp.minimum(squares, clip_limit[:, None, None]), axis=(1, 2))]
  transfers between devices with their start and end apart: 4 -> 5, of which waited for: 2 -> 0; matrix products, arithmetic and copies ran while one was open for 0% -> 2% of each run, Pallas kernels for 0% -> 13%
where the time goes in v1:
time: 62.8 us; the launch traced here: 62.3 us
  blocking collectives  21.4 us (34%)
  Pallas kernels  20.6 us (33%)
  starting transfers between devices  13.4 us (21%)
  local copies, waits for them, and re-layouts  4.99 us (8%)
  other arithmetic  1.85 us (3%)
    all_to_all x2, blocking collectives, shards(): shared = lax.all_to_all(shared, 'strip', 0, 0, tiled=True)  21.4 us
    pallas_call x1, Pallas kernels, shards(): call(middle_kernel, [SMEM, SMEM] + [VMEM] * 4, [((2, chan_count, n_rows,...  8.05 us
    pallas_call x1, Pallas kernels, shards(): call(edge_kernel, [SMEM, SMEM] + [VMEM] * 8, [((2, 4 * chan_count * EDGE,...  7.81 us
    ppermute x2, starting transfers between devices, shards(): into.append(lax.ppermute(rows, ('strip', 'chan'), both))  6.41 us
    ppermute x1, starting transfers between devices, shards(): above = lax.ppermute(sky_cube[:, n_rows - EDGE:], 'strip', down)  5.1 us
    unnamed x12, local copies, waits for them, and re-layouts  3.83 us
    pallas_call x1, Pallas kernels, shards(): call(functools.partial(ratio_kernel, pixels), [SMEM] + [VMEM] * 4, [((cha...  2.79 us
    pallas_call x1, Pallas kernels, shards(): call(functools.partial(clip_kernel, pixels), [VMEM] * 4, [((strips, LANES...  1.95 us
  transfers between devices with their start and end apart: 5, of which 0 were waited for; matrix products, arithmetic and copies ran while one was open for 2% of the time, Pallas kernels for 13%

profile of v1, /device:TPU:0, one launch (start us, length us, event | category | flops | bytes accessed | tf_op | source)
XLA Modules:
  0.0 62.3 jit_solution(4289550003869269442)
XLA Ops:
  0.0 0.7 %subtract_convert_fusion = bf16[16]{0:T(256)(128)(2,1)S(1)} fusion(s32[16]{0:T(128)} %flags.5), kind=kLoop, calls=%fused_computation.2 | loop fusion | flops 32 | bytes 96 | tf_op jit(solution)/shard_map/convert_element_type | solution.py:247
  0.7 0.1 fusion.2
  0.7 1.1 %multiply_select_fusion = bf16[3,64,512]{2,1,0:T(8,128)(2,1)S(1)} fusion(bf16[16,64,512]{2,1,0:T(8,128)(2,1)} %sky.1, pred[]{:T(512)S(6)} %eq.3, bf16[3]{0:T(256)(128)(2,1)S(1)} %get-tuple-element.20, bf16[3]{0:T(256)(128)(2,1)S(1)} %get-tuple-element.19), kind=kLoop, calls=%fused_computation | loop fusion | flops 294912 | bytes 589837 | tf_op jit(solution)/shard_map/jit(_where)/select_n | solution.py:260
  1.9 0.6 collective-permute-start.4
  2.4 1.3 %collective-permute-start.3 = (bf16[3,16,512]{2,1,0:T(8,128)(2,1)S(1)}, bf16[3,16,512]{2,1,0:T(8,128)(2,1)S(1)}, u32[]{:S(2)}, u32[]{:S(2)}) collective-permute-start(bf16[3,16,512]{2,1,0:T(8,128)(2,1)S(1)} %get-tuple-element.17), channel_id=1, source_target_pairs={{2,1},{3,0},{4,3},{5,2},{6,5},{7,4},{8,7},{9,6},{10,9},{11,8},{12,... | collective-permute-start | bytes 147464 | tf_op jit(solution)/shard_map/ppermute | solution.py:271
  3.7 0.0 copy-start.4
  3.7 5.1 %collective-permute-start.2 = (bf16[3,16,512]{2,1,0:T(8,128)(2,1)S(1)}, bf16[3,16,512]{2,1,0:T(8,128)(2,1)S(1)}, u32[]{:S(2)}, u32[]{:S(2)}) collective-permute-start(bf16[3,16,512]{2,1,0:T(8,128)(2,1)S(1)} %get-tuple-element.18), channel_id=1, source_target_pairs={{0,3},{1,2},{2,5},{3,4},{4,7},{5,6},{6,9},{7,8},{8,11},{9,10},{10,... | collective-permute-start | bytes 147464 | tf_op jit(solution)/shard_map/ppermute | solution.py:271
  8.9 1.1 %fusion = (bf16[16,16,512]{2,1,0:T(8,128)(2,1)S(1)}, bf16[16,16,512]{2,1,0:T(8,128)(2,1)S(1)}) fusion(bf16[16,64,512]{2,1,0:T(8,128)(2,1)} %sky.1), kind=kLoop, calls=%fused_computation.3 | loop fusion | bytes 1048576 | tf_op jit(solution)/shard_map/slice | solution.py:253
  9.9 1.3 %collective-permute-start.1 = (bf16[16,16,512]{2,1,0:T(8,128)(2,1)S(1)}, bf16[16,16,512]{2,1,0:T(8,128)(2,1)S(1)}, u32[]{:S(2)}, u32[]{:S(2)}) collective-permute-start(bf16[16,16,512]{2,1,0:T(8,128)(2,1)S(1)} %get-tuple-element.15), channel_id=1, source_target_pairs={{2,0},{4,2},{6,4},{8,6},{10,8},{12,10},{14,12},{3,1},{5,3},{7,5},{... | collective-permute-start | bytes 786440 | tf_op jit(solution)/shard_map/ppermute | solution.py:253
  11.2 5.1 %collective-permute-start = (bf16[16,16,512]{2,1,0:T(8,128)(2,1)S(1)}, bf16[16,16,512]{2,1,0:T(8,128)(2,1)S(1)}, u32[]{:S(2)}, u32[]{:S(2)}) collective-permute-start(bf16[16,16,512]{2,1,0:T(8,128)(2,1)S(1)} %get-tuple-element.16), channel_id=1, source_target_pairs={{0,2},{2,4},{4,6},{6,8},{8,10},{10,12},{12,14},{1,3},{3,5},{5,7},{... | collective-permute-start | bytes 786440 | tf_op jit(solution)/shard_map/ppermute | solution.py:252
  16.3 0.1 add_convert_fusion.sides
  16.4 0.0 collective-permute-done.4
  16.4 0.0 copy-start
  16.4 1.2 %copy-done = bf16[16,64,512]{2,1,0:T(8,128)(2,1)S(1)} copy-done((bf16[16,64,512]{2,1,0:T(8,128)(2,1)S(1)}, bf16[16,64,512]{2,1,0:T(8,128)(2,1)}, u32[]{:S(2)}) %copy-start) | copy-done | bytes 1048600
  17.7 0.0 copy-start.1
  17.7 0.7 %copy-done.1 = s32[16]{0:T(128)S(1)} copy-done((s32[16]{0:T(128)S(1)}, s32[16]{0:T(128)}, u32[]{:S(2)}) %copy-start.1) | copy-done | bytes 88
  18.3 0.0 copy-start.3
  18.3 1.2 %copy-done.3 = bf16[2,512,512]{2,1,0:T(8,128)(2,1)S(1)} copy-done((bf16[2,512,512]{2,1,0:T(8,128)(2,1)S(1)}, bf16[2,512,512]{2,1,0:T(8,128)(2,1)}, u32[]{:S(2)}) %copy-start.3) | copy-done | bytes 1048600
  19.5 0.0 copy-start.5
  19.5 0.7 %copy-done.5 = bf16[64,64]{1,0:T(8,128)(2,1)S(1)} copy-done((bf16[64,64]{1,0:T(8,128)(2,1)S(1)}, bf16[64,64]{1,0:T(8,128)(2,1)}, u32[]{:S(2)}) %copy-start.5) | copy-done | bytes 8216
  20.3 8.1 %middle_rows.1 = (bf16[2,16,64,512]{3,2,1,0:T(8,128)(2,1)S(1)}, f32[2,1024,512]{2,1,0:T(8,128)S(1)}, f32[96,128]{1,0:T(8,128)S(1)}) custom-call(s32[16]{0:T(128)S(1)} %copy-done.1, s32[2]{0:T(128)S(1)} %add_convert_fusion.sides, bf16[16,64,512]{2,1,0:T(8,128)(2,1)S(1)} %copy-done, bf16[1,3,64,512]{3,2,1,0:T(8,128)(2,1)S(1)} %bitcast.17, ...), custom_call_target="tpu_custom_call" | custom-call | flops 2000000000 | bytes 8388608 | tf_op jit(solution)/shard_map/middle_rows/pallas_call | solution.py:300
  28.3 0.0 collective-permute-done.3
  28.3 0.0 collective-permute-done.2
  28.3 0.0 collective-permute-done.1.below
  28.3 0.0 collective-permute-done.above
  28.4 0.0 copy-done.4
  28.4 7.8 %edge_rows.1 = (f32[2,1024,512]{2,1,0:T(8,128)S(1)}, f32[8,128]{1,0:T(8,128)S(1)}) custom-call(s32[16]{0:T(128)S(1)} %copy-done.1, s32[2]{0:T(128)S(1)} %add_convert_fusion.sides, bf16[16,16,512]{2,1,0:T(8,128)(2,1)S(1)} %collective-permute-done.above, bf16[16,16,512]{2,1,0:T(8,128)(2,1)S(1)} %collective-permute-done.1.below, ...), custom_call_target="tpu_custom_call" | custom-call | flops 2000000000 | bytes 8388608 | tf_op jit(solution)/shard_map/edge_rows/pallas_call | solution.py:312
  36.2 12.5 %all_to_all.22 = f32[8,1,128]{2,1,0:T(1,128)S(1)} all-to-all(f32[8,1,128]{2,1,0:T(1,128)S(1)} %bitcast.16), channel_id=1, replica_groups=mesh['groups'=2,'strip'=8,'chan'=2] {'strip'}, dimensions={0} | all-to-all | bytes 8192 | tf_op jit(solution)/shard_map/all_to_all | solution.py:324
  48.7 0.0 copy-start.2
  48.7 2.0 %clip.1 = f32[8,128]{1,0:T(8,128)S(1)} custom-call(f32[8,128]{1,0:T(8,128)S(1)} %bitcast.14, bf16[2,16,64,512]{3,2,1,0:T(8,128)(2,1)S(1)} %get-tuple-element.10.spec, f32[2,1024,512]{2,1,0:T(8,128)S(1)} %get-tuple-element.13.middle, f32[2,1024,512]{2,1,0:T(8,128)S(1)} %get-tuple-element.14.edges), custom_call_target="tpu_custom_call" | custom-call | flops 100000000 | bytes 8388608 | tf_op jit(solution)/shard_map/clip/pallas_call | solution.py:325
  50.6 8.9 %all_to_all.23 = f32[8,1,128]{2,1,0:T(1,128)S(1)} all-to-all(f32[8,1,128]{2,1,0:T(1,128)S(1)} %bitcast.15), channel_id=1, replica_groups=mesh['groups'=2,'strip'=8,'chan'=2] {'strip'}, dimensions={0} | all-to-all | bytes 8192 | tf_op jit(solution)/shard_map/all_to_all | solution.py:333
  59.5 0.0 copy-done.2
  59.5 2.8 %ratio.1 = bf16[16,64,512]{2,1,0:T(8,128)(2,1)} custom-call(s32[16]{0:T(128)S(1)} %copy-done.2, f32[8,128]{1,0:T(8,128)S(1)} %bitcast.13, bf16[2,16,64,512]{3,2,1,0:T(8,128)(2,1)S(1)} %get-tuple-element.10.spec, f32[2,1024,512]{2,1,0:T(8,128)S(1)} %get-tuple-element.13.middle, f32[2,1024,512]{2,1,0:T(8,128)S(1)} %get-tuple-element.14.edges), custom_call_target="tpu_custom_call" | custom-call | flops 100000000 | bytes 8388608 | tf_op jit(solution)/shard_map/ratio/pallas_call | solution.py:334
  (1 shorter events, 0.0 us)
Async XLA Ops:
  1.9 14.6 %collective-permute-start.4 = (bf16[3,64,512]{2,1,0:T(8,128)(2,1)S(1)}, bf16[3,64,512]{2,1,0:T(8,128)(2,1)S(1)}, u32[]{:S(2)}, u32[]{:S(2)}) collective-permute-start(bf16[3,64,512]{2,1,0:T(8,128)(2,1)S(1)} %multiply_select_fusion), channel_id=1, source_target_pairs={{0,1},{1,0},{2,3},{3,2},{4,5},{5,4},{6,7},{7,6},{8,9},{9,8},{10,11... | collective-permute-start | bytes 589832 | tf_op jit(solution)/shard_map/ppermute | solution.py:265
  2.4 25.9 %collective-permute-start.3 = (bf16[3,16,512]{2,1,0:T(8,128)(2,1)S(1)}, bf16[3,16,512]{2,1,0:T(8,128)(2,1)S(1)}, u32[]{:S(2)}, u32[]{:S(2)}) collective-permute-start(bf16[3,16,512]{2,1,0:T(8,128)(2,1)S(1)} %get-tuple-element.17), channel_id=1, source_target_pairs={{2,1},{3,0},{4,3},{5,2},{6,5},{7,4},{8,7},{9,6},{10,9},{11,8},{12,... | collective-permute-start | bytes 147464 | tf_op jit(solution)/shard_map/ppermute | solution.py:271
  3.7 24.6 %copy-start.4 = (bf16[64,96]{1,0:T(8,128)(2,1)S(1)}, bf16[64,96]{1,0:T(8,128)(2,1)}, u32[]{:S(2)}) copy-start(bf16[64,96]{1,0:T(8,128)(2,1)} %constant.20.row_band) | copy-start | bytes 36868
  3.7 24.6 %collective-permute-start.2 = (bf16[3,16,512]{2,1,0:T(8,128)(2,1)S(1)}, bf16[3,16,512]{2,1,0:T(8,128)(2,1)S(1)}, u32[]{:S(2)}, u32[]{:S(2)}) collective-permute-start(bf16[3,16,512]{2,1,0:T(8,128)(2,1)S(1)} %get-tuple-element.18), channel_id=1, source_target_pairs={{0,3},{1,2},{2,5},{3,4},{4,7},{5,6},{6,9},{7,8},{8,11},{9,10},{10,... | collective-permute-start | bytes 147464 | tf_op jit(solution)/shard_map/ppermute | solution.py:271
  9.9 18.4 %collective-permute-start.1 = (bf16[16,16,512]{2,1,0:T(8,128)(2,1)S(1)}, bf16[16,16,512]{2,1,0:T(8,128)(2,1)S(1)}, u32[]{:S(2)}, u32[]{:S(2)}) collective-permute-start(bf16[16,16,512]{2,1,0:T(8,128)(2,1)S(1)} %get-tuple-element.15), channel_id=1, source_target_pairs={{2,0},{4,2},{6,4},{8,6},{10,8},{12,10},{14,12},{3,1},{5,3},{7,5},{... | collective-permute-start | bytes 786440 | tf_op jit(solution)/shard_map/ppermute | solution.py:253
  11.2 17.1 %collective-permute-start = (bf16[16,16,512]{2,1,0:T(8,128)(2,1)S(1)}, bf16[16,16,512]{2,1,0:T(8,128)(2,1)S(1)}, u32[]{:S(2)}, u32[]{:S(2)}) collective-permute-start(bf16[16,16,512]{2,1,0:T(8,128)(2,1)S(1)} %get-tuple-element.16), channel_id=1, source_target_pairs={{0,2},{2,4},{4,6},{6,8},{8,10},{10,12},{12,14},{1,3},{3,5},{5,7},{... | collective-permute-start | bytes 786440 | tf_op jit(solution)/shard_map/ppermute | solution.py:252
  16.4 1.2 %copy-start = (bf16[16,64,512]{2,1,0:T(8,128)(2,1)S(1)}, bf16[16,64,512]{2,1,0:T(8,128)(2,1)}, u32[]{:S(2)}) copy-start(bf16[16,64,512]{2,1,0:T(8,128)(2,1)} %sky.1) | copy-start | bytes 3145732
  17.7 0.7 %copy-start.1 = (s32[16]{0:T(128)S(1)}, s32[16]{0:T(128)}, u32[]{:S(2)}) copy-start(s32[16]{0:T(128)} %flags.5) | copy-start | bytes 196
  18.3 1.2 %copy-start.3 = (bf16[2,512,512]{2,1,0:T(8,128)(2,1)S(1)}, bf16[2,512,512]{2,1,0:T(8,128)(2,1)}, u32[]{:S(2)}) copy-start(bf16[2,512,512]{2,1,0:T(8,128)(2,1)} %constant.19.col_band) | copy-start | bytes 3145732
  19.5 0.7 %copy-start.5 = (bf16[64,64]{1,0:T(8,128)(2,1)S(1)}, bf16[64,64]{1,0:T(8,128)(2,1)}, u32[]{:S(2)}) copy-start(bf16[64,64]{1,0:T(8,128)(2,1)} %constant.18.row_band) | copy-start | bytes 24580
  48.7 10.8 %copy-start.2 = (s32[16]{0:T(128)S(1)}, s32[16]{0:T(128)}, u32[]{:S(2)}) copy-start(s32[16]{0:T(128)} %flags.5) | copy-start | bytes 196

commit v2 on v1

v2 whole, which is shorter than its diff:
```python
import functools
import math

import jax
import jax.numpy as jnp
import numpy as np
from jax import lax
from jax.experimental import pallas as pl
from jax.experimental.pallas import tpu as pltpu
from jax.sharding import PartitionSpec as P

gauss_settings = ((5.0, 8), (10.0, 15))
epsilon = 1e-06
clip_level = 3.0
RIM = 3
REACH = 15
EDGE = 16
LANES = 128
VMEM = pltpu.VMEM
SMEM = pltpu.SMEM


def gauss_weights(fwhm, radius):
    offsets = np.arange(-REACH, REACH + 1)
    spread = fwhm / (2.0 * math.sqrt(2.0 * math.log(2.0)))
    weights = np.exp(-(offsets**2) / (2.0 * spread**2)) * (np.abs(offsets) <= radius)
    weights = weights / weights.sum()
    return weights.astype(np.float32)


def band(out_positions, in_positions):
    offset = np.asarray(in_positions)[None, :] - np.asarray(out_positions)[:, None]
    inside = np.abs(offset) <= REACH
    index = np.clip(offset + REACH, 0, 2 * REACH)
    return np.stack([np.where(inside, gauss_weights(*s)[index], 0.0) for s in gauss_settings])


def constant(matrix):
    return jnp.asarray(matrix.astype(np.float32)).astype(jnp.bfloat16)


def fold(values):
    rows, cols = values.shape
    total = None
    for r in range(0, rows, 8):
        for c in range(0, cols, LANES):
            part = values[r : r + 8, c : c + LANES]
            total = part if total is None else total + part
    return total


def wide(ref, row, rows=EDGE):
    return jnp.broadcast_to(ref[pl.ds(row, 1), :], (rows, LANES))


def spectral_tiles(load, store, chan_count):
    x = [load(c) for c in range(-RIM, chan_count + RIM)]
    for c in range(chan_count):
        s3 = x[c + 2] + x[c + 3] + x[c + 4]
        s7 = (x[c] + x[c + 1]) + s3 + (x[c + 5] + x[c + 6])
        store(0, c, (s3 * (1.0 / 3.0)).astype(jnp.bfloat16))
        store(1, c, (s7 * (1.0 / 7.0)).astype(jnp.bfloat16))


def row_pass(band_ref, plane, rowwise, chan_count, group):
    per = rowwise.shape[1] // (2 * chan_count)

    @pl.loop(0, chan_count // group)
    def _(g):
        for i in range(group):
            c = g * group + i
            for w in range(2):
                row = jnp.dot(band_ref[...], plane(w, c), preferred_element_type=jnp.float32)
                row = row.astype(jnp.bfloat16)
                start = pl.multiple_of((w * chan_count + c) * per, per)
                for f in range(2):
                    rowwise[f, pl.ds(start, per), :] = row[f * per : (f + 1) * per]


def column_pass(rowwise, matrix, out, acc, chan_count):
    n_cols = out.shape[2]
    per = rowwise.shape[1] // (2 * chan_count)
    block = 2 * LANES
    half = LANES
    for f in range(2):
        diagonal = []
        for i, b in enumerate(range(0, n_cols, block)):
            x = rowwise[f, :, b : b + block]
            diagonal.append(jnp.dot(x, matrix[f, i], preferred_element_type=jnp.float32))
        seams = []
        for i, b in enumerate(range(half, n_cols - block, block)):
            x = rowwise[f, :, b : b + block]
            seams.append(
                jnp.dot(x, matrix[f, n_cols // block + i], preferred_element_type=jnp.float32)
            )
        for slot in range(2 * chan_count):
            rows = slice(slot * per, (slot + 1) * per)
            total = None
            for l in range(0, n_cols, LANES):
                b, right = l // block, l % block
                value = diagonal[b][rows, right : right + LANES]
                if right and b < len(seams):
                    value = value + seams[b][rows, :LANES]
                if not right and b > 0:
                    value = value + seams[b - 1][rows, LANES:]
                out[f, rows, l : l + LANES] = value
                part = fold(value * value)
                total = part if total is None else total + part
            w, c = slot // chan_count, slot % chan_count
            acc[(w * 3 + 1 + f) * chan_count + c] = total


def pick_kernel(sky, last_rows, first_rows, sems):
    n_rows = sky.shape[1]
    copies = [
        pltpu.make_async_copy(sky.at[:, n_rows - EDGE :, :], last_rows, sems.at[0]),
        pltpu.make_async_copy(sky.at[:, :EDGE, :], first_rows, sems.at[1]),
    ]
    for copy in copies:
        copy.start()
    for copy in copies:
        copy.wait()


def prepare_kernel(flags, sides, sky, band_in, matrix_in, own, band, matrix, rims, keep, flag, sems):
    chan_count, n_rows, _ = sky.shape
    copies = [
        pltpu.make_async_copy(flags, flag, sems.at[0]),
        pltpu.make_async_copy(sky, own, sems.at[1]),
        pltpu.make_async_copy(matrix_in, matrix, sems.at[2]),
        pltpu.make_async_copy(band_in, band, sems.at[3]),
    ]
    for copy in copies:
        copy.start()
    for copy in copies:
        copy.wait()
    keeps = [(1 - flag[c]).astype(jnp.float32) for c in range(chan_count)]
    for c in range(chan_count):
        keep[c : c + 1, :] = jnp.full((1, LANES), keeps[c], jnp.float32)
    for i in range(2):
        value = jnp.full((1, LANES), sides[i].astype(jnp.float32), jnp.float32)
        keep[chan_count + i : chan_count + i + 1, :] = value
    towards = sides[1].astype(jnp.float32)
    for i in range(RIM):
        tail, head = chan_count - RIM + i, i
        for r in range(0, n_rows, EDGE):
            rows = slice(r, r + EDGE)
            tails = own[tail, rows, :].astype(jnp.float32) * keeps[tail]
            heads = own[head, rows, :].astype(jnp.float32) * keeps[head]
            if rims.shape[0] == 1:
                rims[0, i, rows, :] = (heads + (tails - heads) * towards).astype(jnp.bfloat16)
            else:
                rims[0, i, rows, :] = tails.astype(jnp.bfloat16)
                rims[1, i, rows, :] = heads.astype(jnp.bfloat16)


def corner_kernel(keep, above, below, corners):
    chan_count, _, n_cols = above.shape
    for part, source in enumerate((above, below)):
        for i in range(RIM):
            tail, head = chan_count - RIM + i, i
            for l in range(0, n_cols, LANES):
                cols = slice(l, l + LANES)
                tails = source[tail, :, cols].astype(jnp.float32) * wide(keep, tail)
                heads = source[head, :, cols].astype(jnp.float32) * wide(keep, head)
                if corners.shape[0] == 1:
                    value = heads + (tails - heads) * wide(keep, chan_count + 1)
                    corners[0, part * RIM + i, :, cols] = value.astype(jnp.bfloat16)
                else:
                    corners[0, part * RIM + i, :, cols] = tails.astype(jnp.bfloat16)
                    corners[1, part * RIM + i, :, cols] = heads.astype(jnp.bfloat16)


def middle_kernel(keep, sky, rim, row_band, matrix, spec, smooth, sums, rowwise, acc):
    chan_count, n_rows, n_cols = sky.shape

    @pl.loop(0, n_rows // EDGE)
    def _(t):
        rows = pl.ds(pl.multiple_of(t * EDGE, EDGE), EDGE)
        for lane in range(0, n_cols, LANES):
            cols = slice(lane, lane + LANES)

            def load(c):
                if c < 0:
                    return rim[0, c + RIM, rows, cols].astype(jnp.float32) * wide(keep, chan_count)
                if c >= chan_count:
                    value = rim[rim.shape[0] - 1, c - chan_count, rows, cols].astype(jnp.float32)
                    return value * wide(keep, chan_count + 1)
                return sky[c, rows, cols].astype(jnp.float32) * wide(keep, c)

            def store(w, c, value):
                spec[w, c, rows, cols] = value

            spectral_tiles(load, store, chan_count)

    def plane(w, c):
        value = spec[w, c]
        wide_value = value.astype(jnp.float32)
        acc[w * 3 * chan_count + c] = fold(wide_value * wide_value)
        return value

    row_pass(row_band, plane, rowwise, chan_count, 4)
    column_pass(rowwise, matrix, smooth, acc, chan_count)
    sums[...] = jnp.sum(acc[...], axis=1)


def share(acc_sum, peers):
    rows = acc_sum.shape[0]
    if rows < LANES:
        acc_sum = jnp.concatenate([acc_sum, jnp.zeros((LANES - rows, LANES), jnp.float32)], axis=0)
    total = jnp.sum(acc_sum.T, axis=0, keepdims=True)
    return jnp.broadcast_to(total, (peers, LANES))


def spread(shared):
    total = jnp.sum(shared, axis=0, keepdims=True)
    return jnp.broadcast_to(total, (LANES, LANES)).T


def edge_kernel(
    keep, above, below, corners, spec, row_band, matrix, sums, smooth, shared, rowwise, acc, frame
):
    chan_count, edge, n_cols = above.shape
    n_rows = spec.shape[2]
    for strip, part, base in ((above, 0, 0), (below, RIM, edge + n_rows)):
        for lane in range(0, n_cols, LANES):
            cols = slice(lane, lane + LANES)

            def load(c):
                if c < 0:
                    return corners[0, part + c + RIM, :, cols].astype(jnp.float32) * wide(keep, chan_count)
                if c >= chan_count:
                    value = corners[corners.shape[0] - 1, part + c - chan_count, :, cols].astype(jnp.float32)
                    return value * wide(keep, chan_count + 1)
                return strip[c, :, cols].astype(jnp.float32) * wide(keep, c)

            def store(w, c, value):
                frame[w, c, base : base + edge, cols] = value

            spectral_tiles(load, store, chan_count)
    frame[:, :, edge : edge + n_rows, :] = spec[...]
    row_pass(row_band, lambda w, c: frame[w, c], rowwise, chan_count, 4)
    acc[...] = jnp.zeros_like(acc)
    column_pass(rowwise, matrix, smooth, acc, chan_count)
    shared[...] = share(sums[...] + jnp.sum(acc[...], axis=1), shared.shape[0])


def clip_kernel(pixels, shared_in, spec, middle, edges, shared, limit, acc):
    chan_count = spec.shape[1]
    rough = jnp.sqrt(spread(shared_in[...]) / pixels + epsilon)
    limit[...] = (clip_level * rough) ** 2
    per = middle.shape[1] // (2 * chan_count)

    @pl.loop(0, chan_count)
    def _(c):
        for w in range(2):
            start = pl.multiple_of((w * chan_count + c) * per, per)
            for f in range(-1, 2):
                slot = (w * 3 + 1 + f) * chan_count + c
                top = jnp.broadcast_to(limit[pl.ds(slot, 1), :], (8, LANES))
                total = None
                if f < 0:
                    parts = [spec[w, c].astype(jnp.float32)]
                else:
                    parts = [middle[f, pl.ds(start, per), :], edges[f, pl.ds(start, per), :]]
                for part in parts:
                    for r in range(0, part.shape[0], 8):
                        for l in range(0, part.shape[1], LANES):
                            value = part[r : r + 8, l : l + LANES]
                            value = jnp.minimum(value * value, top)
                            total = value if total is None else total + value
                acc[slot] = total

    shared[...] = share(jnp.sum(acc[...], axis=1), shared.shape[0])


def ratio_kernel(pixels, keep, shared_in, spec, middle, edges, out, scale, staged, sems):
    chan_count, n_rows, n_cols = out.shape
    edge = EDGE
    scale[...] = 1.0 / jnp.sqrt(spread(shared_in[...]) / pixels + epsilon)
    per = middle.shape[1] // (2 * chan_count)
    parts = sems.shape[0]
    group = chan_count // parts

    def channel(c):
        keep_tile = wide(keep, c)
        factors = [wide(scale, k * chan_count + c) for k in range(6)]
        for r in range(0, n_rows, 16):
            if r < edge:
                source, offset = edges, r
            elif r < n_rows - edge:
                source, offset = middle, r - edge
            else:
                source, offset = edges, r - (n_rows - edge) + edge
            for l in range(0, n_cols, LANES):
                cols = slice(l, l + LANES)
                best = None
                for w in range(2):
                    values = [spec[w, c, r : r + 16, cols].astype(jnp.float32)]
                    start = pl.multiple_of((w * chan_count + c) * per + offset, 16)
                    values += [source[f, pl.ds(start, 16), cols] for f in range(2)]
                    for f in range(3):
                        value = values[f] * factors[w * 3 + f]
                        best = value if best is None else jnp.maximum(best, value)
                staged[c, r : r + 16, cols] = (best * keep_tile).astype(jnp.bfloat16)

    copies = []
    for p in range(parts):
        pl.loop(p * group, (p + 1) * group)(channel)
        s = slice(p * group, (p + 1) * group)
        copies.append(pltpu.make_async_copy(staged.at[s], out.at[s], sems.at[p]))
        copies[-1].start()
    for copy in copies:
        copy.wait()


def specs(spaces):
    return [pl.BlockSpec(memory_space=s) for s in spaces]


def shards(sky_cube, chan_flags):
    chan_count, n_rows, n_cols = sky_cube.shape
    strips, blocks = lax.axis_size("strip"), lax.axis_size("chan")
    pixels = n_rows * strips * n_cols
    block = lax.axis_index("chan")
    f32, bf16 = jnp.float32, jnp.bfloat16
    slots = 6 * chan_count
    mid = n_rows - 2 * EDGE
    turns = 1 if blocks == 2 else 2

    def call(kernel, ins, outs, scratch, flops, out_spaces=None):
        return pl.pallas_call(
            kernel,
            in_specs=specs(ins),
            out_specs=specs(out_spaces or [VMEM] * len(outs)),
            out_shape=[jax.ShapeDtypeStruct(s, d) for s, d in outs],
            scratch_shapes=scratch,
            compiler_params=pltpu.CompilerParams(vmem_limit_bytes=32 * 2**20),
            cost_estimate=pl.CostEstimate(flops=flops, bytes_accessed=8 * 2**20, transcendentals=0),
        )

    own_rows = np.arange(n_rows)
    mid_band = constant(band(own_rows[EDGE : n_rows - EDGE], own_rows).reshape(2 * mid, n_rows))
    edge_rows = np.concatenate([own_rows[:EDGE], own_rows[n_rows - EDGE :]])
    framed = np.arange(-EDGE, n_rows + EDGE)
    edge_band = constant(band(edge_rows, framed).reshape(4 * EDGE, n_rows + 2 * EDGE))
    cols = np.arange(n_cols)
    matrix = band(cols, cols).transpose(0, 2, 1)
    side = 2 * LANES
    same = cols[:, None] // side == cols[None, :] // side
    starts = np.arange(0, n_cols, side)
    pieces = [(matrix * same)[:, b : b + side, b : b + side] for b in starts]
    pieces += [(matrix * ~same)[:, b : b + side, b : b + side] for b in starts[:-1] + LANES]
    matrix = constant(np.stack(pieces, axis=1))

    sky_cube = pltpu.with_memory_space_constraint(sky_cube, pltpu.HBM)
    chan_flags = pltpu.with_memory_space_constraint(chan_flags, pltpu.HBM)
    matrix = pltpu.with_memory_space_constraint(matrix, pltpu.HBM)
    mid_band = pltpu.with_memory_space_constraint(mid_band, pltpu.HBM)

    rows_block = ((chan_count, EDGE, n_cols), bf16)
    last_rows, first_rows = call(
        pick_kernel, [pltpu.HBM], [rows_block, rows_block], [pltpu.SemaphoreType.DMA((2,))], 10**6
    )(sky_cube)

    onward = [(i, i + 1) for i in range(strips - 1)]
    backward = [(j, i) for i, j in onward]
    above = lax.ppermute(last_rows, "strip", onward)
    below = lax.ppermute(first_rows, "strip", backward)

    sides = jnp.stack([block > 0, block < blocks - 1]).astype(jnp.int32)
    own, mid_band, matrix, rims, keep = call(
        prepare_kernel,
        [pltpu.HBM, SMEM, pltpu.HBM, pltpu.HBM, pltpu.HBM],
        [
            ((chan_count, n_rows, n_cols), bf16),
            (mid_band.shape, bf16),
            (matrix.shape, bf16),
            ((turns, RIM, n_rows, n_cols), bf16),
            ((chan_count + 8, LANES), f32),
        ],
        [SMEM((chan_count,), jnp.int32), pltpu.SemaphoreType.DMA((4,))],
        10**6,
    )(chan_flags, sides, sky_cube, mid_band, matrix)

    forth = [(i, i + 1) for i in range(blocks - 1)]
    back = [(j, i) for i, j in forth]
    moves = [forth + back] if blocks == 2 else [forth, back]

    def across(payload):
        sent = [lax.ppermute(payload[i : i + 1], "chan", p) for i, p in enumerate(moves)]
        return jnp.concatenate(sent)

    rim = across(rims)
    spec, middle, sums = call(
        middle_kernel,
        [VMEM] * 5,
        [
            ((2, chan_count, n_rows, n_cols), bf16),
            ((2, 2 * chan_count * mid, n_cols), f32),
            ((slots, LANES), f32),
        ],
        [VMEM((2, 2 * chan_count * mid, n_cols), bf16), VMEM((slots, 8, LANES), f32)],
        2 * 10**9,
    )(keep, own, rim, mid_band, matrix)

    (corners,) = call(
        corner_kernel, [VMEM] * 3, [((turns, 2 * RIM, EDGE, n_cols), bf16)], [], 10**6
    )(keep, above, below)
    corners = across(corners)

    edges, shared = call(
        edge_kernel,
        [VMEM] * 8,
        [((2, 4 * chan_count * EDGE, n_cols), f32), ((strips, LANES), f32)],
        [
            VMEM((2, 4 * chan_count * EDGE, n_cols), bf16),
            VMEM((slots, 8, LANES), f32),
            VMEM((2, chan_count, n_rows + 2 * EDGE, n_cols), bf16),
        ],
        2 * 10**9,
    )(keep, above, below, corners, spec, edge_band, matrix, sums)
    shared = lax.all_to_all(shared, "strip", 0, 0, tiled=True)
    (shared,) = call(
        functools.partial(clip_kernel, pixels),
        [VMEM] * 4,
        [((strips, LANES), f32)],
        [VMEM((LANES, LANES), f32), VMEM((slots, 8, LANES), f32)],
        10**8,
    )(shared, spec, middle, edges)
    shared = lax.all_to_all(shared, "strip", 0, 0, tiled=True)
    (out,) = call(
        functools.partial(ratio_kernel, pixels),
        [VMEM] * 5,
        [((chan_count, n_rows, n_cols), bf16)],
        [
            VMEM((LANES, LANES), f32),
            VMEM((chan_count, n_rows, n_cols), bf16),
            pltpu.SemaphoreType.DMA((4,)),
        ],
        10**8,
        [pltpu.HBM],
    )(keep, shared, spec, middle, edges)
    return out


def solution(mesh):
    in_specs = (P("chan", "strip", "groups"), P("chan"))
    out_specs = P("chan", "strip", "groups")
    return jax.shard_map(shards, mesh=mesh, in_specs=in_specs, out_specs=out_specs, check_vma=False)
```

time: 62.8 us -> 49.1 us (0.78)
  Pallas kernels: 20.6 us -> 12.9 us
  waiting for transfers between devices: 0.01 us -> 7.55 us
  starting transfers between devices: 13.4 us -> 6.32 us
  local copies, waits for them, and re-layouts: 4.99 us -> 0.01 us
  other arithmetic: 1.85 us -> 0.08 us
    pallas_call x3 -> x6, Pallas kernels: 18.7 us -> 10.9 us  [the longest x1 2.91 us: shards(): call(middle_kernel, [VMEM] * 5, [((2, chan_count, n_rows, n_cols), bf16),...]
    ppermute x5 -> x4, waiting for transfers between devices: 0.01 us -> 7.55 us  [the longest x1 7.54 us: shards(): above = lax.ppermute(last_rows, 'strip', onward)]
    ppermute x5 -> x4, starting transfers between devices: 13.4 us -> 6.32 us  [the longest x1 4.89 us: shards(): above = lax.ppermute(last_rows, 'strip', onward)]
    unnamed x12 -> x2, local copies, waits for them, and re-layouts: 3.83 us -> 0.01 us
    slice x3 -> x0, local copies, waits for them, and re-layouts: 1.16 us -> none  [the longest x1 1.07 us: shards(): below = lax.ppermute(sky_cube[:, :EDGE], 'strip', up)]
    select_n x1 -> x0, other arithmetic: 1.11 us -> none  [shards(): moves = [(jnp.where(block == 0, last, first), forth + back)]]
    convert_element_type x1 -> x0, other arithmetic: 0.66 us -> none  [shards(): keep_mask = (1 - chan_flags).astype(jnp.bfloat16)]
  transfers between devices with their start and end apart: 5 -> 4, of which waited for: 0 -> 1; matrix products, arithmetic and copies ran while one was open for 2% -> 0% of each run, Pallas kernels for 13% -> 10%
where the time goes in v2:
time: 49.1 us; the launch traced here: 48.8 us
  blocking collectives  21.9 us (45%)
  Pallas kernels  12.9 us (26%)
  waiting for transfers between devices  7.55 us (15%)
  starting transfers between devices  6.32 us (13%)
    all_to_all x2, blocking collectives, shards(): shared = lax.all_to_all(shared, 'strip', 0, 0, tiled=True)  21.9 us
    ppermute x1, waiting for transfers between devices, shards(): above = lax.ppermute(last_rows, 'strip', onward)  7.54 us
    ppermute x1, starting transfers between devices, shards(): above = lax.ppermute(last_rows, 'strip', onward)  4.89 us
    pallas_call x1, Pallas kernels, shards(): call(middle_kernel, [VMEM] * 5, [((2, chan_count, n_rows, n_cols), bf16),...  2.91 us
    pallas_call x1, Pallas kernels, shards(): call(edge_kernel, [VMEM] * 8, [((2, 4 * chan_count * EDGE, n_cols), f32),...  2.68 us
    pallas_call x1, Pallas kernels, shards(): call(prepare_kernel, [pltpu.HBM, SMEM, pltpu.HBM, pltpu.HBM, pltpu.HBM],...  2.13 us
    pallas_call x1, Pallas kernels, shards(): call(functools.partial(ratio_kernel, pixels), [VMEM] * 5, [((chan_count,...  2.09 us
    pallas_call x1, Pallas kernels, shards(): call(functools.partial(clip_kernel, pixels), [VMEM] * 4, [((strips, LANES...  1.96 us
  transfers between devices with their start and end apart: 4, of which 1 were waited for; matrix products, arithmetic and copies ran while one was open for 0% of the time, Pallas kernels for 10%

profile of v2, /device:TPU:0, one launch (start us, length us, event | category | flops | bytes accessed | tf_op | source)
XLA Modules:
  0.0 48.8 jit_solution(11634742421215645966)
XLA Ops:
  0.0 1.0 %shard_map.56 = (bf16[16,16,512]{2,1,0:T(8,128)(2,1)S(1)}, bf16[16,16,512]{2,1,0:T(8,128)(2,1)S(1)}) custom-call(bf16[16,64,512]{2,1,0:T(8,128)(2,1)} %sky.3), custom_call_target="tpu_custom_call" | custom-call | flops 1000000 | bytes 8388608 | tf_op jit(solution)/shard_map/pallas_call | solution.py:362
  1.1 4.9 %collective-permute-start = (bf16[16,16,512]{2,1,0:T(8,128)(2,1)S(1)}, bf16[16,16,512]{2,1,0:T(8,128)(2,1)S(1)}, u32[]{:S(2)}, u32[]{:S(2)}) collective-permute-start(bf16[16,16,512]{2,1,0:T(8,128)(2,1)S(1)} %get-tuple-element.18), channel_id=1, source_target_pairs={{0,2},{2,4},{4,6},{6,8},{8,10},{10,12},{12,14},{1,3},{3,5},{5,7},{... | collective-permute-start | bytes 786440 | tf_op jit(solution)/shard_map/ppermute | solution.py:368
  5.9 1.3 %collective-permute-start.1 = (bf16[16,16,512]{2,1,0:T(8,128)(2,1)S(1)}, bf16[16,16,512]{2,1,0:T(8,128)(2,1)S(1)}, u32[]{:S(2)}, u32[]{:S(2)}) collective-permute-start(bf16[16,16,512]{2,1,0:T(8,128)(2,1)S(1)} %get-tuple-element.19), channel_id=1, source_target_pairs={{2,0},{4,2},{6,4},{8,6},{10,8},{12,10},{14,12},{3,1},{5,3},{7,5},{... | collective-permute-start | bytes 786440 | tf_op jit(solution)/shard_map/ppermute | solution.py:369
  7.3 0.1 add_convert_fusion.sides
  7.3 2.1 %shard_map.55 = (bf16[16,64,512]{2,1,0:T(8,128)(2,1)S(1)}, bf16[64,64]{1,0:T(8,128)(2,1)S(1)}, bf16[2,3,256,256]{3,2,1,0:T(8,128)(2,1)S(1)}, bf16[1,3,64,512]{3,2,1,0:T(8,128)(2,1)S(1)}, f32[24,128]{1,0:T(8,128)S(1)}) custom-call(s32[16]{0:T(128)} %flags.1, s32[2]{0:T(128)S(1)} %add_convert_fusion.sides, bf16[16,64,512]{2,1,0:T(8,128)(2,1)} %sky.3, ...), custom_call_target="tpu_custom_call" | custom-call | flops 1000000 | bytes 8388608 | tf_op jit(solution)/shard_map/pallas_call | solution.py:372
  9.5 0.0 copy-start
  9.5 0.1 collective-permute-start.3
  9.6 7.5 %collective-permute-done.above = bf16[16,16,512]{2,1,0:T(8,128)(2,1)S(1)} collective-permute-done((bf16[16,16,512]{2,1,0:T(8,128)(2,1)S(1)}, bf16[16,16,512]{2,1,0:T(8,128)(2,1)S(1)}, u32[]{:S(2)}, u32[]{:S(2)}) %collective-permute-start) | collective-permute-done | bytes 262176 | tf_op jit(solution)/shard_map/ppermute | solution.py:368
  17.1 0.0 collective-permute-done.1.below
  17.1 0.1 shard_map.57
  17.2 0.1 collective-permute-start.2
  17.2 0.0 collective-permute-done.3.rim
  17.2 2.9 %shard_map.58 = (bf16[2,16,64,512]{3,2,1,0:T(8,128)(2,1)S(1)}, f32[2,1024,512]{2,1,0:T(8,128)S(1)}, f32[96,128]{1,0:T(8,128)S(1)}) custom-call(f32[24,128]{1,0:T(8,128)S(1)} %get-tuple-element.17.keep, bf16[16,64,512]{2,1,0:T(8,128)(2,1)S(1)} %get-tuple-element.20.sky, bf16[1,3,64,512]{3,2,1,0:T(8,128)(2,1)S(1)} %collective-permute-done.3.rim, ...), custom_call_target="tpu_custom_call" | custom-call | flops 2000000000 | bytes 8388608 | tf_op jit(solution)/shard_map/pallas_call | solution.py:395
  20.2 0.0 collective-permute-done.2.corners
  20.2 0.0 copy-done
  20.2 2.7 %shard_map.59 = (f32[2,1024,512]{2,1,0:T(8,128)S(1)}, f32[8,128]{1,0:T(8,128)S(1)}) custom-call(f32[24,128]{1,0:T(8,128)S(1)} %get-tuple-element.17.keep, bf16[16,16,512]{2,1,0:T(8,128)(2,1)S(1)} %collective-permute-done.above, bf16[16,16,512]{2,1,0:T(8,128)(2,1)S(1)} %collective-permute-done.1.below, ...), custom_call_target="tpu_custom_call" | custom-call | flops 2000000000 | bytes 8388608 | tf_op jit(solution)/shard_map/pallas_call | solution.py:412
  22.9 13.1 %all_to_all.22 = f32[8,1,128]{2,1,0:T(1,128)S(1)} all-to-all(f32[8,1,128]{2,1,0:T(1,128)S(1)} %bitcast.13), channel_id=1, replica_groups=mesh['groups'=2,'strip'=8,'chan'=2] {'strip'}, dimensions={0} | all-to-all | bytes 8192 | tf_op jit(solution)/shard_map/all_to_all | solution.py:423
  35.9 2.0 %shard_map.60 = f32[8,128]{1,0:T(8,128)S(1)} custom-call(f32[8,128]{1,0:T(8,128)S(1)} %bitcast.11, bf16[2,16,64,512]{3,2,1,0:T(8,128)(2,1)S(1)} %get-tuple-element.24.spec, f32[2,1024,512]{2,1,0:T(8,128)S(1)} %get-tuple-element.27.middle, f32[2,1024,512]{2,1,0:T(8,128)S(1)} %get-tuple-element.28.edges), custom_call_target="tpu_custom_call" | custom-call | flops 100000000 | bytes 8388608 | tf_op jit(solution)/shard_map/pallas_call | solution.py:424
  37.9 8.9 %all_to_all.23 = f32[8,1,128]{2,1,0:T(1,128)S(1)} all-to-all(f32[8,1,128]{2,1,0:T(1,128)S(1)} %bitcast.12), channel_id=1, replica_groups=mesh['groups'=2,'strip'=8,'chan'=2] {'strip'}, dimensions={0} | all-to-all | bytes 8192 | tf_op jit(solution)/shard_map/all_to_all | solution.py:431
  46.7 2.1 %shard_map.61 = bf16[16,64,512]{2,1,0:T(8,128)(2,1)} custom-call(f32[24,128]{1,0:T(8,128)S(1)} %get-tuple-element.17.keep, f32[8,128]{1,0:T(8,128)S(1)} %bitcast.10, bf16[2,16,64,512]{3,2,1,0:T(8,128)(2,1)S(1)} %get-tuple-element.24.spec, f32[2,1024,512]{2,1,0:T(8,128)S(1)} %get-tuple-element.27.middle, f32[2,1024,512]{2,1,0:T(8,128)S(1)} %get-tuple-element.28.edges), custom_call_target="tpu_custom_call" | custom-call | flops 100000000 | bytes 8388608 | tf_op jit(solution)/shard_map/pallas_call | solution.py:432
Async XLA Ops:
  1.1 16.0 %collective-permute-start = (bf16[16,16,512]{2,1,0:T(8,128)(2,1)S(1)}, bf16[16,16,512]{2,1,0:T(8,128)(2,1)S(1)}, u32[]{:S(2)}, u32[]{:S(2)}) collective-permute-start(bf16[16,16,512]{2,1,0:T(8,128)(2,1)S(1)} %get-tuple-element.18), channel_id=1, source_target_pairs={{0,2},{2,4},{4,6},{6,8},{8,10},{10,12},{12,14},{1,3},{3,5},{5,7},{... | collective-permute-start | bytes 786440 | tf_op jit(solution)/shard_map/ppermute | solution.py:368
  5.9 11.2 %collective-permute-start.1 = (bf16[16,16,512]{2,1,0:T(8,128)(2,1)S(1)}, bf16[16,16,512]{2,1,0:T(8,128)(2,1)S(1)}, u32[]{:S(2)}, u32[]{:S(2)}) collective-permute-start(bf16[16,16,512]{2,1,0:T(8,128)(2,1)S(1)} %get-tuple-element.19), channel_id=1, source_target_pairs={{2,0},{4,2},{6,4},{8,6},{10,8},{12,10},{14,12},{3,1},{5,3},{7,5},{... | collective-permute-start | bytes 786440 | tf_op jit(solution)/shard_map/ppermute | solution.py:369
  9.5 10.7 %copy-start = (bf16[64,96]{1,0:T(8,128)(2,1)S(1)}, bf16[64,96]{1,0:T(8,128)(2,1)}, u32[]{:S(2)}) copy-start(bf16[64,96]{1,0:T(8,128)(2,1)} %constant.19.row_band) | copy-start | bytes 36868
  9.5 7.8 %collective-permute-start.3 = (bf16[1,3,64,512]{3,2,1,0:T(8,128)(2,1)S(1)}, bf16[1,3,64,512]{3,2,1,0:T(8,128)(2,1)S(1)}, u32[]{:S(2)}, u32[]{:S(2)}) collective-permute-start(bf16[1,3,64,512]{3,2,1,0:T(8,128)(2,1)S(1)} %get-tuple-element.21), channel_id=1, source_target_pairs={{0,1},{1,0},{2,3},{3,2},{4,5},{5,4},{6,7},{7,6},{8,9},{9,8},{10,11... | collective-permute-start | bytes 589832 | tf_op jit(solution)/shard_map/ppermute | solution.py:391
  17.2 3.0 %collective-permute-start.2 = (bf16[1,6,16,512]{3,2,1,0:T(8,128)(2,1)S(1)}, bf16[1,6,16,512]{3,2,1,0:T(8,128)(2,1)S(1)}, u32[]{:S(2)}, u32[]{:S(2)}) collective-permute-start(bf16[1,6,16,512]{3,2,1,0:T(8,128)(2,1)S(1)} %shard_map.57), channel_id=1, source_target_pairs={{0,1},{1,0},{2,3},{3,2},{4,5},{5,4},{6,7},{7,6},{8,9},{9,8},{10,11... | collective-permute-start | bytes 294920 | tf_op jit(solution)/shard_map/ppermute | solution.py:391

commit v3 on v0

v3 whole, which is shorter than its diff:
```python
import functools
import math

import jax
import jax.numpy as jnp
import numpy as np
from jax import lax
from jax.experimental import pallas as pl
from jax.experimental.pallas import tpu as pltpu
from jax.sharding import PartitionSpec as P

gauss_settings = ((5.0, 8), (10.0, 15))
epsilon = 1e-06
clip_level = 3.0
RIM = 3
REACH = 15
EDGE = 16
LANES = 128
BLOCK = 2 * LANES
VMEM, HBM, SMEM = pltpu.VMEM, pltpu.HBM, pltpu.SMEM
f32, bf16 = jnp.float32, jnp.bfloat16


def gauss_weights(fwhm, radius):
    offsets = np.arange(-REACH, REACH + 1)
    spread = fwhm / (2.0 * math.sqrt(2.0 * math.log(2.0)))
    weights = np.exp(-(offsets**2) / (2.0 * spread**2)) * (np.abs(offsets) <= radius)
    weights = weights / weights.sum()
    return weights.astype(np.float32)


def band(out_positions, in_positions):
    offset = np.asarray(in_positions)[None, :] - np.asarray(out_positions)[:, None]
    inside = np.abs(offset) <= REACH
    index = np.clip(offset + REACH, 0, 2 * REACH)
    return np.stack([np.where(inside, gauss_weights(*s)[index], 0.0) for s in gauss_settings])


def constant(matrix):
    return jnp.asarray(matrix.astype(np.float32)).astype(bf16)


def fold(values):
    rows, cols = values.shape
    total = None
    for r in range(0, rows, 8):
        for c in range(0, cols, LANES):
            part = values[r : r + 8, c : c + LANES]
            total = part if total is None else total + part
    return total


def wide(ref, row, rows=EDGE):
    return jnp.broadcast_to(ref[pl.ds(row, 1), :], (rows, LANES))


def towards(chan_count, turns):
    last = chan_count - RIM
    if turns == 1:
        return [jnp.where(lax.axis_index("chan") == 0, last, 0)]
    return [last, 0]


def pair_rows(n_rows, pair):
    odd = lax.rem(lax.axis_index("strip"), 2)
    at_end = odd == pair
    return pl.multiple_of(jnp.where(at_end, n_rows - EDGE, 0), EDGE)


def spectral_slot(chan_count, w, c):
    return w * chan_count + c


def smooth_slot(chan_count, w, f, c):
    return (2 + 2 * w + f) * chan_count + c


def spectral_tiles(load, store, chan_count):
    x = [load(c) for c in range(-RIM, chan_count + RIM)]
    for c in range(chan_count):
        s3 = x[c + 2] + x[c + 3] + x[c + 4]
        s7 = (x[c] + x[c + 1]) + s3 + (x[c + 5] + x[c + 6])
        store(0, c, (s3 * (1.0 / 3.0)).astype(bf16))
        store(1, c, (s7 * (1.0 / 7.0)).astype(bf16))


def spectral_rows(keep, body, rim, store, chan_count, n_cols, rows):
    for lane in range(0, n_cols, LANES):
        cols = slice(lane, lane + LANES)

        def load(c):
            if c < 0:
                value, row = rim[0, c + RIM, rows, cols], chan_count
            elif c >= chan_count:
                value, row = rim[rim.shape[0] - 1, c - chan_count, rows, cols], chan_count + 1
            else:
                value, row = body[c, rows, cols], c
            return value.astype(f32) * wide(keep, row)

        spectral_tiles(load, functools.partial(store, cols), chan_count)


def row_pass(row_band, plane, rowwise, chan_count, group):
    per = rowwise.shape[1] // (2 * chan_count)

    @pl.loop(0, chan_count // group)
    def _(g):
        taps = row_band()
        for i in range(group):
            c = g * group + i
            for w in range(2):
                row = jnp.dot(taps, plane(w, c), preferred_element_type=f32).astype(bf16)
                start = pl.multiple_of((w * chan_count + c) * per, per)
                for f in range(2):
                    rowwise[f, pl.ds(start, per), :] = row[f * per : (f + 1) * per]


def column_pass(rowwise, matrix, out, add, chan_count):
    n_cols = out.shape[2]
    per = rowwise.shape[1] // (2 * chan_count)
    blocks = n_cols // BLOCK
    for f in range(2):
        products = []
        for i in range(2 * blocks - 1):
            b = i * BLOCK if i < blocks else (i - blocks) * BLOCK + LANES
            x = rowwise[f, :, b : b + BLOCK]
            products.append(jnp.dot(x, matrix[f, i], preferred_element_type=f32))
        diagonal, seams = products[:blocks], products[blocks:]
        for slot in range(2 * chan_count):
            rows = slice(slot * per, (slot + 1) * per)
            total = None
            for l in range(0, n_cols, LANES):
                b, right = l // BLOCK, l % BLOCK
                value = diagonal[b][rows, right : right + LANES]
                if right and b < len(seams):
                    value = value + seams[b][rows, :LANES]
                if not right and b > 0:
                    value = value + seams[b - 1][rows, LANES:]
                out[f, rows, l : l + LANES] = value
                part = fold(value * value)
                total = part if total is None else total + part
            add(slot // chan_count, f, slot % chan_count, total)


def run(copies):
    for copy in copies:
        copy.start()
    for copy in copies:
        copy.wait()


def pick_kernel(sky, first_pair, second_pair, sems):
    pieces = (first_pair, second_pair)
    rows = [pl.ds(pair_rows(sky.shape[1], pair), EDGE) for pair in range(2)]
    run(
        [
            pltpu.make_async_copy(sky.at[:, rows[pair], :], pieces[pair], sems.at[pair])
            for pair in range(2)
        ]
    )


def rim_kernel(flags, sky, rims, keep, flag, raw, sems):
    chan_count, _, _ = sky.shape
    turns = rims.shape[0]
    first = towards(chan_count, turns)
    copies = [pltpu.make_async_copy(flags, flag, sems.at[turns])]
    for turn in range(turns):
        source = sky.at[pl.ds(first[turn], RIM)]
        copies.append(pltpu.make_async_copy(source, raw.at[turn], sems.at[turn]))
    run(copies)
    for c in range(chan_count):
        keep[c : c + 1, :] = jnp.full((1, LANES), (1 - flag[c]).astype(f32), f32)
    block = lax.axis_index("chan")
    for i, inside in enumerate((block > 0, block < lax.axis_size("chan") - 1)):
        value = jnp.full((1, LANES), inside.astype(jnp.int32).astype(f32), f32)
        keep[chan_count + i : chan_count + i + 1, :] = value
    for turn in range(turns):
        for i in range(RIM):
            factor = (1 - flag[first[turn] + i]).astype(f32)
            rims[turn, i] = (raw[turn, i].astype(f32) * factor).astype(bf16)


def load_kernel(sky, mid_in, edge_in, matrix_in, own, mid_band, edge_band, matrix, sems):
    run(
        [
            pltpu.make_async_copy(sky, own, sems.at[0]),
            pltpu.make_async_copy(matrix_in, matrix, sems.at[1]),
            pltpu.make_async_copy(mid_in, mid_band, sems.at[2]),
            pltpu.make_async_copy(edge_in, edge_band, sems.at[3]),
        ]
    )


def corner_kernel(keep, halo, corners):
    chan_count, _, n_cols = halo.shape
    for turn, first in enumerate(towards(chan_count, corners.shape[0])):
        for i in range(RIM):
            factor = wide(keep, first + i)
            for l in range(0, n_cols, LANES):
                cols = slice(l, l + LANES)
                corners[turn, i, :, cols] = (halo[first + i, :, cols].astype(f32) * factor).astype(bf16)


def middle_kernel(keep, sky, rim, row_band, matrix, spec, smooth, sums, rowwise, acc):
    chan_count, n_rows, n_cols = sky.shape

    @pl.loop(0, n_rows // EDGE)
    def _(t):
        rows = pl.ds(pl.multiple_of(t * EDGE, EDGE), EDGE)

        def store(cols, w, c, value):
            spec[w, c, rows, cols] = value

        spectral_rows(keep, sky, rim, store, chan_count, n_cols, rows)

    def plane(w, c):
        value = spec[w, c]
        exact = value.astype(f32)
        acc[spectral_slot(chan_count, w, c)] = fold(exact * exact)
        return value

    def add(w, f, c, total):
        acc[smooth_slot(chan_count, w, f, c)] = total

    row_pass(lambda: row_band[...], plane, rowwise, chan_count, 4)
    column_pass(rowwise, matrix, smooth, add, chan_count)
    sums[...] = jnp.sum(acc[...], axis=1)


def edge_kernel(pair, keep, halo, corners, spec, row_band, matrix, sums, smooth, sums_out, rowwise, acc, frame):
    chan_count, n_rows, n_cols = spec.shape[1:]
    at = pair_rows(n_rows, pair)
    near = frame.shape[2] - EDGE

    def store(cols, w, c, value):
        frame[w, c, :EDGE, cols] = value

    spectral_rows(keep, halo, corners, store, chan_count, n_cols, slice(None))
    inner = pl.multiple_of(jnp.where(at == 0, 0, n_rows - near), EDGE)
    frame[:, :, EDGE:, :] = spec[:, :, pl.ds(inner, near), :]
    which = jnp.where(at == 0, 0, 1)

    def add(w, f, c, total):
        acc[smooth_slot(chan_count, w, f, c) - 2 * chan_count] = total

    row_pass(lambda: row_band[which], lambda w, c: frame[w, c], rowwise, chan_count, 4)
    column_pass(rowwise, matrix, smooth, add, chan_count)
    before = sums[: 2 * chan_count, :]
    total = sums[2 * chan_count :, :] + jnp.sum(acc[...], axis=1)
    if pair == 0:
        sums_out[: 2 * chan_count, :] = before
        sums_out[2 * chan_count :, :] = total
    else:
        sums_out[...] = share(jnp.concatenate([before, total]), sums_out)


def share(acc_sum, out):
    peers, width = out.shape
    slots = acc_sum.shape[0]
    if slots < width:
        acc_sum = jnp.concatenate([acc_sum, jnp.zeros((width - slots, LANES), f32)], axis=0)
    total = jnp.sum(acc_sum.T, axis=0, keepdims=True)
    return jnp.broadcast_to(total, (peers, width))


def spread(shared):
    total = jnp.sum(shared[...], axis=0, keepdims=True)
    return jnp.broadcast_to(total, (LANES, total.shape[1])).T


def clip_kernel(pixels, shared_in, spec, middle, edge_one, edge_two, shared, limit, acc):
    chan_count = spec.shape[1]
    rough = jnp.sqrt(spread(shared_in) / pixels + epsilon)
    limit[...] = (clip_level * rough) ** 2

    @pl.loop(0, chan_count)
    def _(c):
        def clipped(slot, parts):
            top = wide(limit, slot, 8)
            total = None
            for part in parts:
                for r in range(0, part.shape[0], 8):
                    for l in range(0, part.shape[1], LANES):
                        value = part[r : r + 8, l : l + LANES]
                        value = jnp.minimum(value * value, top)
                        total = value if total is None else total + value
            acc[slot] = total

        for w in range(2):
            clipped(spectral_slot(chan_count, w, c), [spec[w, c].astype(f32)])
            for f in range(2):
                parts = []
                for source in (middle, edge_one, edge_two):
                    per = source.shape[1] // (2 * chan_count)
                    start = pl.multiple_of((w * chan_count + c) * per, per)
                    parts.append(source[f, pl.ds(start, per), :])
                clipped(smooth_slot(chan_count, w, f, c), parts)

    shared[...] = share(jnp.sum(acc[...], axis=1), shared)


def ratio_kernel(pixels, keep, shared_in, spec, middle, edge_one, edge_two, out, scale, staged, sems):
    chan_count, n_rows, n_cols = out.shape
    scale[...] = 1.0 / jnp.sqrt(spread(shared_in) / pixels + epsilon)
    parts = sems.shape[0]
    group = chan_count // parts
    tiles = [(middle, r, EDGE + r) for r in range(0, n_rows - 2 * EDGE, EDGE)]
    tiles += [(edge_one, 0, pair_rows(n_rows, 0)), (edge_two, 0, pair_rows(n_rows, 1))]

    def channel(c):
        keep_tile = wide(keep, c)
        factors = [
            [wide(scale, spectral_slot(chan_count, w, c))]
            + [wide(scale, smooth_slot(chan_count, w, f, c)) for f in range(2)]
            for w in range(2)
        ]
        for source, offset, row in tiles:
            rows = pl.ds(row, EDGE)
            per = source.shape[1] // (2 * chan_count)
            for l in range(0, n_cols, LANES):
                cols = slice(l, l + LANES)
                best = None
                for w in range(2):
                    start = pl.multiple_of((w * chan_count + c) * per + offset, EDGE)
                    values = [spec[w, c, rows, cols].astype(f32)]
                    values += [source[f, pl.ds(start, EDGE), cols] for f in range(2)]
                    for value, factor in zip(values, factors[w]):
                        value = value * factor
                        best = value if best is None else jnp.maximum(best, value)
                staged[c, rows, cols] = (best * keep_tile).astype(bf16)

    copies = []
    for p in range(parts):
        pl.loop(p * group, (p + 1) * group)(channel)
        s = slice(p * group, (p + 1) * group)
        copies.append(pltpu.make_async_copy(staged.at[s], out.at[s], sems.at[p]))
        copies[-1].start()
    for copy in copies:
        copy.wait()


def specs(spaces):
    return [pl.BlockSpec(memory_space=s) for s in spaces]


def call(kernel, ins, outs, scratch, flops, out_space=VMEM):
    return pl.pallas_call(
        kernel,
        in_specs=specs(ins),
        out_specs=specs([out_space] * len(outs)),
        out_shape=[jax.ShapeDtypeStruct(s, d) for s, d in outs],
        scratch_shapes=scratch,
        compiler_params=pltpu.CompilerParams(vmem_limit_bytes=32 * 2**20),
        cost_estimate=pl.CostEstimate(flops=flops, bytes_accessed=2**20, transcendentals=0),
    )


def shards(sky_cube, chan_flags):
    chan_count, n_rows, n_cols = sky_cube.shape
    strips, blocks = lax.axis_size("strip"), lax.axis_size("chan")
    pixels = n_rows * strips * n_cols
    turns = 1 if blocks == 2 else 2
    slots = 6 * chan_count
    width = -(-slots // LANES) * LANES
    mid = n_rows - 2 * EDGE
    near = 2 * EDGE
    dma = pltpu.SemaphoreType.DMA

    own_rows = np.arange(n_rows)
    mid_band = constant(band(own_rows[EDGE : n_rows - EDGE], own_rows).reshape(2 * mid, n_rows))
    top = band(np.arange(EDGE), np.concatenate([np.arange(-EDGE, 0), np.arange(near)]))
    bottom = band(np.arange(near - EDGE, near), np.concatenate([np.arange(near, near + EDGE), np.arange(near)]))
    edge_band = constant(np.stack([top, bottom]).reshape(2, 2 * EDGE, EDGE + near))
    cols = np.arange(n_cols)
    taps = band(cols, cols).transpose(0, 2, 1)
    same = cols[:, None] // BLOCK == cols[None, :] // BLOCK
    starts = np.arange(0, n_cols, BLOCK)
    pieces = [(taps * same)[:, b : b + BLOCK, b : b + BLOCK] for b in starts]
    pieces += [(taps * ~same)[:, b : b + BLOCK, b : b + BLOCK] for b in starts[:-1] + LANES]
    matrix = constant(np.stack(pieces, axis=1))

    sky_cube, chan_flags, mid_band, edge_band, matrix = (
        pltpu.with_memory_space_constraint(v, HBM)
        for v in (sky_cube, chan_flags, mid_band, edge_band, matrix)
    )

    edge_rows = ((chan_count, EDGE, n_cols), bf16)
    first_pair, second_pair = call(
        pick_kernel, [HBM], [edge_rows, edge_rows], [dma((2,))], 10**6
    )(sky_cube)

    evens = [(i, i + 1) for i in range(0, strips - 1, 2)]
    odds = [(i, i + 1) for i in range(1, strips - 1, 2)]
    evens, odds = (p + [(b, a) for a, b in p] for p in (evens, odds))
    first_pair = lax.ppermute(first_pair, "strip", evens)
    second_pair = lax.ppermute(second_pair, "strip", odds)

    forth = [(i, i + 1) for i in range(blocks - 1)]
    back = [(j, i) for i, j in forth]
    moves = [forth + back] if turns == 1 else [forth, back]

    def across(payload):
        sent = [lax.ppermute(payload[i : i + 1], "chan", p) for i, p in enumerate(moves)]
        return jnp.concatenate(sent)

    rims, keep = call(
        rim_kernel,
        [HBM, HBM],
        [((turns, RIM, n_rows, n_cols), bf16), ((chan_count + 8, LANES), f32)],
        [
            SMEM((chan_count,), jnp.int32),
            VMEM((turns, RIM, n_rows, n_cols), bf16),
            dma((turns + 1,)),
        ],
        10**6,
    )(chan_flags, sky_cube)
    rim = across(rims)
    own, mid_band, edge_band, matrix = call(
        load_kernel,
        [HBM] * 4,
        [(v.shape, bf16) for v in (sky_cube, mid_band, edge_band, matrix)],
        [dma((4,))],
        10**6,
    )(sky_cube, mid_band, edge_band, matrix)

    def corners_of(halo):
        (corners,) = call(
            corner_kernel, [VMEM] * 2, [((turns, RIM, EDGE, n_cols), bf16)], [], 10**6
        )(keep, halo)
        return across(corners)

    corners_one = corners_of(first_pair)
    corners_two = corners_of(second_pair)
    spec, middle, sums = call(
        middle_kernel,
        [VMEM] * 5,
        [
            ((2, chan_count, n_rows, n_cols), bf16),
            ((2, 2 * chan_count * mid, n_cols), f32),
            ((slots, LANES), f32),
        ],
        [VMEM((2, 2 * chan_count * mid, n_cols), bf16), VMEM((slots, 8, LANES), f32)],
        2 * 10**9,
    )(keep, own, rim, mid_band, matrix)

    edge_out = ((2, 2 * chan_count * EDGE, n_cols), f32)
    edge_scratch = [
        VMEM((2, 2 * chan_count * EDGE, n_cols), bf16),
        VMEM((slots - 2 * chan_count, 8, LANES), f32),
        VMEM((2, chan_count, EDGE + near, n_cols), bf16),
    ]
    edge_one, sums = call(
        functools.partial(edge_kernel, 0),
        [VMEM] * 7,
        [edge_out, ((slots, LANES), f32)],
        edge_scratch,
        10**9,
    )(keep, first_pair, corners_one, spec, edge_band, matrix, sums)
    edge_two, shared = call(
        functools.partial(edge_kernel, 1),
        [VMEM] * 7,
        [edge_out, ((strips, width), f32)],
        edge_scratch,
        10**9,
    )(keep, second_pair, corners_two, spec, edge_band, matrix, sums)

    shared = lax.all_to_all(shared, "strip", 0, 0, tiled=True)
    (shared,) = call(
        functools.partial(clip_kernel, pixels),
        [VMEM] * 5,
        [((strips, width), f32)],
        [VMEM((width, LANES), f32), VMEM((slots, 8, LANES), f32)],
        10**8,
    )(shared, spec, middle, edge_one, edge_two)
    shared = lax.all_to_all(shared, "strip", 0, 0, tiled=True)
    (out,) = call(
        functools.partial(ratio_kernel, pixels),
        [VMEM] * 6,
        [((chan_count, n_rows, n_cols), bf16)],
        [VMEM((width, LANES), f32), VMEM((chan_count, n_rows, n_cols), bf16), dma((4,))],
        10**8,
        HBM,
    )(keep, shared, spec, middle, edge_one, edge_two)
    return out


def solution(mesh):
    in_specs = (P("chan", "strip", "groups"), P("chan"))
    out_specs = P("chan", "strip", "groups")
    return jax.shard_map(shards, mesh=mesh, in_specs=in_specs, out_specs=out_specs, check_vma=False)
```

time: 95.6 us -> 47.5 us (0.50)
  blocking collectives: 38.9 us -> 20.9 us
  other arithmetic: 14.2 us -> 0 us
  Pallas kernels: 0 us -> 13.9 us
  matrix products: 11 us -> 0 us
  waiting for transfers between devices: 16.4 us -> 7.96 us
  local copies, waits for them, and re-layouts: 5.26 us -> 0 us
  starting transfers between devices: 9.23 us -> 4.4 us
    psum x2 -> x0, blocking collectives: 38.9 us -> none  [the longest x1 21.8 us: shards(): total_power = lax.psum(jnp.sum(squares, axis=(1, 2)), 'strip')]
    all_to_all x0 -> x2, blocking collectives: none -> 20.9 us  [shards(): shared = lax.all_to_all(shared, 'strip', 0, 0, tiled=True)]
    pallas_call x0 -> x10, Pallas kernels: none -> 13.9 us  [the longest x1 2.91 us: shards(): call(middle_kernel, [VMEM] * 5, [((2, chan_count, n_rows, n_cols), bf16),...]
    dot_general x8 -> x0, matrix products: 11 us -> none  [the longest x4 9.33 us: column_pass(): result = jnp.dot(joined, matrix, preferred_element_type=jnp.float32)]
    ppermute x4 -> x5, waiting for transfers between devices: 16.4 us -> 7.96 us  [the longest x1 7.95 us: shards(): first_pair = lax.ppermute(first_pair, 'strip', evens)]
    convert_element_type x3 -> x0, other arithmetic: 7.96 us -> none  [the longest x1 5.19 us: shards(): (peak_ratio * keep_mask.astype(jnp.float32)[:, None, None]).astype(jnp.bf...]
    ppermute x4 -> x5, starting transfers between devices: 9.23 us -> 4.4 us  [the longest x1 3.03 us: shards(): first_pair = lax.ppermute(first_pair, 'strip', evens)]
    reduce_sum x7 -> x0, other arithmetic: 3.5 us -> none  [the longest x6 2.66 us: shards(): jnp.sum(jnp.minimum(squares, clip_limit[:, None, None]), axis=(1, 2))]
  transfers between devices with their start and end apart: 4 -> 5, of which waited for: 2 -> 1; matrix products, arithmetic and copies ran while one was open for 0% -> 0% of each run, Pallas kernels for 0% -> 15%
where the time goes in v3:
time: 47.5 us; the launch traced here: 47.2 us
  blocking collectives  20.9 us (44%)
  Pallas kernels  13.9 us (29%)
  waiting for transfers between devices  7.96 us (17%)
  starting transfers between devices  4.4 us (9%)
    all_to_all x2, blocking collectives, shards(): shared = lax.all_to_all(shared, 'strip', 0, 0, tiled=True)  20.9 us
    ppermute x1, waiting for transfers between devices, shards(): first_pair = lax.ppermute(first_pair, 'strip', evens)  7.95 us
    ppermute x1, starting transfers between devices, shards(): first_pair = lax.ppermute(first_pair, 'strip', evens)  3.03 us
    pallas_call x1, Pallas kernels, shards(): call(middle_kernel, [VMEM] * 5, [((2, chan_count, n_rows, n_cols), bf16),...  2.91 us
    pallas_call x1, Pallas kernels, shards(): call(functools.partial(ratio_kernel, pixels), [VMEM] * 6, [((chan_count,...  2.09 us
    pallas_call x1, Pallas kernels, shards(): call(functools.partial(clip_kernel, pixels), [VMEM] * 5, [((strips, width...  1.98 us
    pallas_call x1, Pallas kernels, shards(): call(functools.partial(edge_kernel, 1), [VMEM] * 7, [edge_out, ((strips,...  1.71 us
    pallas_call x1, Pallas kernels, shards(): call(functools.partial(edge_kernel, 0), [VMEM] * 7, [edge_out, ((slots, L...  1.63 us
  transfers between devices with their start and end apart: 5, of which 1 were waited for; matrix products, arithmetic and copies ran while one was open for 0% of the time, Pallas kernels for 15%

profile of v3, /device:TPU:0, one launch (start us, length us, event | category | flops | bytes accessed | tf_op | source)
XLA Modules:
  0.0 47.2 jit_solution(13035521265154883952)
XLA Ops:
  0.0 1.0 %shard_map.56 = (bf16[16,16,512]{2,1,0:T(8,128)(2,1)S(1)}, bf16[16,16,512]{2,1,0:T(8,128)(2,1)S(1)}) custom-call(bf16[16,64,512]{2,1,0:T(8,128)(2,1)} %sky.5), custom_call_target="tpu_custom_call" | custom-call | flops 1000000 | bytes 1048576 | tf_op jit(solution)/shard_map/pallas_call | solution.py:389
  1.1 3.0 %collective-permute-start.3 = (bf16[16,16,512]{2,1,0:T(8,128)(2,1)S(1)}, bf16[16,16,512]{2,1,0:T(8,128)(2,1)S(1)}, u32[]{:S(2)}, u32[]{:S(2)}) collective-permute-start(bf16[16,16,512]{2,1,0:T(8,128)(2,1)S(1)} %get-tuple-element.28), channel_id=1, source_target_pairs={{0,2},{4,6},{8,10},{12,14},{2,0},{6,4},{10,8},{14,12},{1,3},{5,7},... | collective-permute-start | bytes 786440 | tf_op jit(solution)/shard_map/ppermute | solution.py:396
  4.1 1.0 %shard_map.55 = (bf16[1,3,64,512]{3,2,1,0:T(8,128)(2,1)S(1)}, f32[24,128]{1,0:T(8,128)S(1)}) custom-call(s32[16]{0:T(128)} %flags.1, bf16[16,64,512]{2,1,0:T(8,128)(2,1)} %sky.5), custom_call_target="tpu_custom_call" | custom-call | flops 1000000 | bytes 1048576 | tf_op jit(solution)/shard_map/pallas_call | solution.py:407
  5.1 0.1 collective-permute-start.2
  5.2 0.7 %collective-permute-start = (bf16[16,16,512]{2,1,0:T(8,128)(2,1)S(1)}, bf16[16,16,512]{2,1,0:T(8,128)(2,1)S(1)}, u32[]{:S(2)}, u32[]{:S(2)}) collective-permute-start(bf16[16,16,512]{2,1,0:T(8,128)(2,1)S(1)} %get-tuple-element.21), channel_id=1, source_target_pairs={{2,4},{6,8},{10,12},{4,2},{8,6},{12,10},{3,5},{7,9},{11,13},{5,3},... | collective-permute-start | bytes 786440 | tf_op jit(solution)/shard_map/ppermute | solution.py:397
  5.8 1.5 %shard_map.58 = (bf16[16,64,512]{2,1,0:T(8,128)(2,1)S(1)}, bf16[64,64]{1,0:T(8,128)(2,1)S(1)}, bf16[2,32,48]{2,1,0:T(8,128)(2,1)S(1)}, bf16[2,3,256,256]{3,2,1,0:T(8,128)(2,1)S(1)}) custom-call(bf16[16,64,512]{2,1,0:T(8,128)(2,1)} %sky.5, bf16[64,64]{1,0:T(8,128)(2,1)} %constant.9.mid_in, bf16[2,32,48]{2,1,0:T(8,128)(2,1)} %constant.10.edge_in, ...), custom_call_target="tpu_custom_call" | custom-call | flops 1000000 | bytes 1048576 | tf_op jit(solution)/shard_map/pallas_call | solution.py:419
  7.3 8.0 %collective-permute-done.3.halo = bf16[16,16,512]{2,1,0:T(8,128)(2,1)S(1)} collective-permute-done((bf16[16,16,512]{2,1,0:T(8,128)(2,1)S(1)}, bf16[16,16,512]{2,1,0:T(8,128)(2,1)S(1)}, u32[]{:S(2)}, u32[]{:S(2)}) %collective-permute-start.3) | collective-permute-done | bytes 262176 | tf_op jit(solution)/shard_map/ppermute | solution.py:396
  15.3 0.1 collective-permute-start.4
  15.4 0.0 collective-permute-done.2.rim
  15.4 2.9 %shard_map.59 = (bf16[2,16,64,512]{3,2,1,0:T(8,128)(2,1)S(1)}, f32[2,1024,512]{2,1,0:T(8,128)S(1)}, f32[96,128]{1,0:T(8,128)S(1)}) custom-call(f32[24,128]{1,0:T(8,128)S(1)} %get-tuple-element.20.keep, bf16[16,64,512]{2,1,0:T(8,128)(2,1)S(1)} %get-tuple-element.22.sky, bf16[1,3,64,512]{3,2,1,0:T(8,128)(2,1)S(1)} %collective-permute-done.2.rim, ...), custom_call_target="tpu_custom_call" | custom-call | flops 2000000000 | bytes 1048576 | tf_op jit(solution)/shard_map/pallas_call | solution.py:435
  18.3 0.0 collective-permute-done.halo
  18.4 0.5 %collective-permute-start.1 = (bf16[1,3,16,512]{3,2,1,0:T(8,128)(2,1)S(1)}, bf16[1,3,16,512]{3,2,1,0:T(8,128)(2,1)S(1)}, u32[]{:S(2)}, u32[]{:S(2)}) collective-permute-start(bf16[1,3,16,512]{3,2,1,0:T(8,128)(2,1)S(1)} %shard_map.57), channel_id=1, source_target_pairs={{0,1},{1,0},{2,3},{3,2},{4,5},{5,4},{6,7},{7,6},{8,9},{9,8},{10,11... | collective-permute-start | bytes 147464 | tf_op jit(solution)/shard_map/ppermute | solution.py:404
  18.9 0.0 collective-permute-done.4.corners
  18.9 1.6 %shard_map.61 = (f32[2,512,512]{2,1,0:T(8,128)S(1)}, f32[96,128]{1,0:T(8,128)S(1)}) custom-call(f32[24,128]{1,0:T(8,128)S(1)} %get-tuple-element.20.keep, bf16[16,16,512]{2,1,0:T(8,128)(2,1)S(1)} %collective-permute-done.3.halo, bf16[1,3,16,512]{3,2,1,0:T(8,128)(2,1)S(1)} %collective-permute-done.4.corners, ...), custom_call_target="tpu_custom_call" | custom-call | flops 1000000000 | bytes 1048576 | tf_op jit(solution)/shard_map/pallas_call | solution.py:453
  20.5 0.0 collective-permute-done.1.corners
  20.6 1.7 %shard_map.62 = (f32[2,512,512]{2,1,0:T(8,128)S(1)}, f32[8,128]{1,0:T(8,128)S(1)}) custom-call(f32[24,128]{1,0:T(8,128)S(1)} %get-tuple-element.20.keep, bf16[16,16,512]{2,1,0:T(8,128)(2,1)S(1)} %collective-permute-done.halo, bf16[1,3,16,512]{3,2,1,0:T(8,128)(2,1)S(1)} %collective-permute-done.1.corners, ...), custom_call_target="tpu_custom_call" | custom-call | flops 1000000000 | bytes 1048576 | tf_op jit(solution)/shard_map/pallas_call | solution.py:460
  22.3 12.0 %all_to_all.22 = f32[8,1,128]{2,1,0:T(1,128)S(1)} all-to-all(f32[8,1,128]{2,1,0:T(1,128)S(1)} %bitcast.11), channel_id=1, replica_groups=mesh['groups'=2,'strip'=8,'chan'=2] {'strip'}, dimensions={0} | all-to-all | bytes 8192 | tf_op jit(solution)/shard_map/all_to_all | solution.py:468
  34.3 2.0 %shard_map.63 = f32[8,128]{1,0:T(8,128)S(1)} custom-call(f32[8,128]{1,0:T(8,128)S(1)} %bitcast.9, bf16[2,16,64,512]{3,2,1,0:T(8,128)(2,1)S(1)} %get-tuple-element.26.spec, f32[2,1024,512]{2,1,0:T(8,128)S(1)} %get-tuple-element.32.middle, f32[2,512,512]{2,1,0:T(8,128)S(1)} %get-tuple-element.33.edge_one, f32[2,512,512]{2,1,0:T(8,128)S(1)} %get-tuple-element.34.edge_two), custom_call_target="tpu_custom_call" | custom-call | flops 100000000 | bytes 1048576 | tf_op jit(solution)/shard_map/pallas_call | solution.py:469
  36.3 8.9 %all_to_all.23 = f32[8,1,128]{2,1,0:T(1,128)S(1)} all-to-all(f32[8,1,128]{2,1,0:T(1,128)S(1)} %bitcast.10), channel_id=1, replica_groups=mesh['groups'=2,'strip'=8,'chan'=2] {'strip'}, dimensions={0} | all-to-all | bytes 8192 | tf_op jit(solution)/shard_map/all_to_all | solution.py:476
  45.2 2.1 %shard_map.64 = bf16[16,64,512]{2,1,0:T(8,128)(2,1)} custom-call(f32[24,128]{1,0:T(8,128)S(1)} %get-tuple-element.20.keep, f32[8,128]{1,0:T(8,128)S(1)} %bitcast.8, bf16[2,16,64,512]{3,2,1,0:T(8,128)(2,1)S(1)} %get-tuple-element.26.spec, f32[2,1024,512]{2,1,0:T(8,128)S(1)} %get-tuple-element.32.middle, f32[2,512,512]{2,1,0:T(8,128)S(1)} %get-tuple-element.33.edge_one, ...), custom_call_target="tpu_custom_call" | custom-call | flops 100000000 | bytes 1048576 | tf_op jit(solution)/shard_map/pallas_call | solution.py:477
  (2 shorter events, 0.0 us)
Async XLA Ops:
  1.1 14.2 %collective-permute-start.3 = (bf16[16,16,512]{2,1,0:T(8,128)(2,1)S(1)}, bf16[16,16,512]{2,1,0:T(8,128)(2,1)S(1)}, u32[]{:S(2)}, u32[]{:S(2)}) collective-permute-start(bf16[16,16,512]{2,1,0:T(8,128)(2,1)S(1)} %get-tuple-element.28), channel_id=1, source_target_pairs={{0,2},{4,6},{8,10},{12,14},{2,0},{6,4},{10,8},{14,12},{1,3},{5,7},... | collective-permute-start | bytes 786440 | tf_op jit(solution)/shard_map/ppermute | solution.py:396
  5.1 10.3 %collective-permute-start.2 = (bf16[1,3,64,512]{3,2,1,0:T(8,128)(2,1)S(1)}, bf16[1,3,64,512]{3,2,1,0:T(8,128)(2,1)S(1)}, u32[]{:S(2)}, u32[]{:S(2)}) collective-permute-start(bf16[1,3,64,512]{3,2,1,0:T(8,128)(2,1)S(1)} %get-tuple-element.23), channel_id=1, source_target_pairs={{0,1},{1,0},{2,3},{3,2},{4,5},{5,4},{6,7},{7,6},{8,9},{9,8},{10,11... | collective-permute-start | bytes 589832 | tf_op jit(solution)/shard_map/ppermute | solution.py:404
  5.2 13.2 %collective-permute-start = (bf16[16,16,512]{2,1,0:T(8,128)(2,1)S(1)}, bf16[16,16,512]{2,1,0:T(8,128)(2,1)S(1)}, u32[]{:S(2)}, u32[]{:S(2)}) collective-permute-start(bf16[16,16,512]{2,1,0:T(8,128)(2,1)S(1)} %get-tuple-element.21), channel_id=1, source_target_pairs={{2,4},{6,8},{10,12},{4,2},{8,6},{12,10},{3,5},{7,9},{11,13},{5,3},... | collective-permute-start | bytes 786440 | tf_op jit(solution)/shard_map/ppermute | solution.py:397
  15.3 3.6 %collective-permute-start.4 = (bf16[1,3,16,512]{3,2,1,0:T(8,128)(2,1)S(1)}, bf16[1,3,16,512]{3,2,1,0:T(8,128)(2,1)S(1)}, u32[]{:S(2)}, u32[]{:S(2)}) collective-permute-start(bf16[1,3,16,512]{3,2,1,0:T(8,128)(2,1)S(1)} %shard_map.60), channel_id=1, source_target_pairs={{0,1},{1,0},{2,3},{3,2},{4,5},{5,4},{6,7},{7,6},{8,9},{9,8},{10,11... | collective-permute-start | bytes 147464 | tf_op jit(solution)/shard_map/ppermute | solution.py:404
  18.4 2.2 %collective-permute-start.1 = (bf16[1,3,16,512]{3,2,1,0:T(8,128)(2,1)S(1)}, bf16[1,3,16,512]{3,2,1,0:T(8,128)(2,1)S(1)}, u32[]{:S(2)}, u32[]{:S(2)}) collective-permute-start(bf16[1,3,16,512]{3,2,1,0:T(8,128)(2,1)S(1)} %shard_map.57), channel_id=1, source_target_pairs={{0,1},{1,0},{2,3},{3,2},{4,5},{5,4},{6,7},{7,6},{8,9},{9,8},{10,11... | collective-permute-start | bytes 147464 | tf_op jit(solution)/shard_map/ppermute | solution.py:404

commit v4 on v3

--- a/solution.py
+++ b/solution.py
@@ -61,6 +61,12 @@
     return [last, 0]
 
 
+def rest(chan_count, turns):
+    if turns == 1:
+        return jnp.where(lax.axis_index("chan") == 0, 0, RIM), chan_count - RIM
+    return RIM, chan_count - 2 * RIM
+
+
 def pair_rows(n_rows, pair):
     odd = lax.rem(lax.axis_index("strip"), 2)
     at_end = odd == pair
@@ -75,49 +81,27 @@
     return (2 + 2 * w + f) * chan_count + c
 
 
-def spectral_tiles(load, store, chan_count):
-    x = [load(c) for c in range(-RIM, chan_count + RIM)]
-    for c in range(chan_count):
-        s3 = x[c + 2] + x[c + 3] + x[c + 4]
-        s7 = (x[c] + x[c + 1]) + s3 + (x[c + 5] + x[c + 6])
-        store(0, c, (s3 * (1.0 / 3.0)).astype(bf16))
-        store(1, c, (s7 * (1.0 / 7.0)).astype(bf16))
-
-
-def spectral_rows(keep, body, rim, store, chan_count, n_cols, rows):
-    for lane in range(0, n_cols, LANES):
-        cols = slice(lane, lane + LANES)
-
-        def load(c):
-            if c < 0:
-                value, row = rim[0, c + RIM, rows, cols], chan_count
-            elif c >= chan_count:
-                value, row = rim[rim.shape[0] - 1, c - chan_count, rows, cols], chan_count + 1
-            else:
-                value, row = body[c, rows, cols], c
-            return value.astype(f32) * wide(keep, row)
-
-        spectral_tiles(load, functools.partial(store, cols), chan_count)
-
-
-def row_pass(row_band, plane, rowwise, chan_count, group):
-    per = rowwise.shape[1] // (2 * chan_count)
-
-    @pl.loop(0, chan_count // group)
-    def _(g):
-        taps = row_band()
-        for i in range(group):
-            c = g * group + i
-            for w in range(2):
-                row = jnp.dot(taps, plane(w, c), preferred_element_type=f32).astype(bf16)
-                start = pl.multiple_of((w * chan_count + c) * per, per)
-                for f in range(2):
-                    rowwise[f, pl.ds(start, per), :] = row[f * per : (f + 1) * per]
-
-
-def column_pass(rowwise, matrix, out, add, chan_count):
-    n_cols = out.shape[2]
-    per = rowwise.shape[1] // (2 * chan_count)
+def means(x):
+    for i in range(RIM, len(x) - RIM):
+        s3 = x[i - 1] + x[i] + x[i + 1]
+        s7 = (x[i - 3] + x[i - 2]) + s3 + (x[i + 2] + x[i + 3])
+        yield i - RIM, [(s3 * (1.0 / 3.0)).astype(bf16), (s7 * (1.0 / 7.0)).astype(bf16)]
+
+
+def row_pass(taps, plane, rowwise, slots, count, at=0):
+    per = taps.shape[0] // 2
+    for i in range(count):
+        row = jnp.dot(taps, plane(slots[i]), preferred_element_type=f32).astype(bf16)
+        start = (at + i) * per
+        if not isinstance(start, int):
+            start = pl.multiple_of(start, per)
+        for f in range(2):
+            rowwise[f, pl.ds(start, per), :] = row[f * per : (f + 1) * per]
+
+
+def column_pass(rowwise, matrix, count, put):
+    n_cols = rowwise.shape[2]
+    per = rowwise.shape[1] // count
     blocks = n_cols // BLOCK
     for f in range(2):
         products = []
@@ -126,9 +110,9 @@
             x = rowwise[f, :, b : b + BLOCK]
             products.append(jnp.dot(x, matrix[f, i], preferred_element_type=f32))
         diagonal, seams = products[:blocks], products[blocks:]
-        for slot in range(2 * chan_count):
+        for slot in range(count):
             rows = slice(slot * per, (slot + 1) * per)
-            total = None
+            values = []
             for l in range(0, n_cols, LANES):
                 b, right = l // BLOCK, l % BLOCK
                 value = diagonal[b][rows, right : right + LANES]
@@ -136,10 +120,21 @@
                     value = value + seams[b][rows, :LANES]
                 if not right and b > 0:
                     value = value + seams[b - 1][rows, LANES:]
-                out[f, rows, l : l + LANES] = value
-                part = fold(value * value)
-                total = part if total is None else total + part
-            add(slot // chan_count, f, slot % chan_count, total)
+                values.append(value)
+            put(f, slot, values)
+
+
+def put_tiles(smooth, squares, acc, f, start, slot, values):
+    rows = pl.ds(start, values[0].shape[0])
+    total = None
+    for i, value in enumerate(values):
+        cols = slice(i * LANES, (i + 1) * LANES)
+        square = value * value
+        smooth[f, rows, cols] = value
+        squares[f, rows, cols] = square
+        part = fold(square)
+        total = part if total is None else total + part
+    acc[slot] = total
 
 
 def run(copies):
@@ -169,12 +164,12 @@
         source = sky.at[pl.ds(first[turn], RIM)]
         copies.append(pltpu.make_async_copy(source, raw.at[turn], sems.at[turn]))
     run(copies)
-    for c in range(chan_count):
-        keep[c : c + 1, :] = jnp.full((1, LANES), (1 - flag[c]).astype(f32), f32)
     block = lax.axis_index("chan")
-    for i, inside in enumerate((block > 0, block < lax.axis_size("chan") - 1)):
-        value = jnp.full((1, LANES), inside.astype(jnp.int32).astype(f32), f32)
-        keep[chan_count + i : chan_count + i + 1, :] = value
+    before = (block > 0).astype(jnp.int32)
+    after = (block < lax.axis_size("chan") - 1).astype(jnp.int32)
+    factors = [before] * RIM + [1 - flag[c] for c in range(chan_count)] + [after] * RIM
+    for i, factor in enumerate(factors):
+        keep[i : i + 1, :] = jnp.full((1, LANES), factor.astype(f32), f32)
     for turn in range(turns):
         for i in range(RIM):
             factor = (1 - flag[first[turn] + i]).astype(f32)
@@ -196,63 +191,117 @@
     chan_count, _, n_cols = halo.shape
     for turn, first in enumerate(towards(chan_count, corners.shape[0])):
         for i in range(RIM):
-            factor = wide(keep, first + i)
+            factor = wide(keep, RIM + first + i)
             for l in range(0, n_cols, LANES):
                 cols = slice(l, l + LANES)
                 corners[turn, i, :, cols] = (halo[first + i, :, cols].astype(f32) * factor).astype(bf16)
 
 
-def middle_kernel(keep, sky, rim, row_band, matrix, spec, smooth, sums, rowwise, acc):
+def middle_kernel(keep, sky, rim, row_band, matrix, spec, spec_squares, smooth, squares, sums, rowwise, acc):
     chan_count, n_rows, n_cols = sky.shape
+    per = n_rows - 2 * EDGE
 
     @pl.loop(0, n_rows // EDGE)
     def _(t):
         rows = pl.ds(pl.multiple_of(t * EDGE, EDGE), EDGE)
-
-        def store(cols, w, c, value):
-            spec[w, c, rows, cols] = value
-
-        spectral_rows(keep, sky, rim, store, chan_count, n_cols, rows)
-
-    def plane(w, c):
-        value = spec[w, c]
-        exact = value.astype(f32)
-        acc[spectral_slot(chan_count, w, c)] = fold(exact * exact)
-        return value
-
-    def add(w, f, c, total):
-        acc[smooth_slot(chan_count, w, f, c)] = total
-
-    row_pass(lambda: row_band[...], plane, rowwise, chan_count, 4)
-    column_pass(rowwise, matrix, smooth, add, chan_count)
+        for lane in range(0, n_cols, LANES):
+            cols = slice(lane, lane + LANES)
+            x = [rim[0, i, rows, cols] for i in range(RIM)]
+            x += [sky[c, rows, cols] for c in range(chan_count)]
+            x += [rim[rim.shape[0] - 1, i, rows, cols] for i in range(RIM)]
+            x = [value.astype(f32) * wide(keep, i) for i, value in enumerate(x)]
+            for c, both in means(x):
+                for w in range(2):
+                    spec[w, c, rows, cols] = both[w]
+
+    group = 4
+
+    @pl.loop(0, chan_count // group)
+    def _(g):
+        for w in range(2):
+
+            def plane(c):
+                value = spec[w, c]
+                exact = value.astype(f32)
+                square = exact * exact
+                spec_squares[w, c] = square
+                acc[spectral_slot(chan_count, w, c)] = fold(square)
+                return value
+
+            c = [g * group + i for i in range(group)]
+            row_pass(row_band[...], plane, rowwise, c, group, w * chan_count + g * group)
+
+    def put(f, slot, values):
+        w, c = slot // chan_count, slot % chan_count
+        target = smooth_slot(chan_count, w, f, c)
+        put_tiles(smooth, squares, acc, f, slot * per, target, values)
+
+    column_pass(rowwise, matrix, 2 * chan_count, put)
     sums[...] = jnp.sum(acc[...], axis=1)
 
 
-def edge_kernel(pair, keep, halo, corners, spec, row_band, matrix, sums, smooth, sums_out, rowwise, acc, frame):
+def edge_kernel(pair, turns, inner, rims, peers, *refs):
+    refs = list(refs)
+    keep, halo = refs[:2]
+    del refs[:2]
+    corners = refs.pop(0) if rims else None
+    spec, row_band, matrix, sums = refs[:4]
+    if rims and not inner:
+        del refs[4:6]
+    smooth, squares, sums_out, rowwise, acc, frame = refs[-6:]
     chan_count, n_rows, n_cols = spec.shape[1:]
+    near = frame.shape[2] - EDGE
     at = pair_rows(n_rows, pair)
-    near = frame.shape[2] - EDGE
-
-    def store(cols, w, c, value):
-        frame[w, c, :EDGE, cols] = value
-
-    spectral_rows(keep, halo, corners, store, chan_count, n_cols, slice(None))
-    inner = pl.multiple_of(jnp.where(at == 0, 0, n_rows - near), EDGE)
-    frame[:, :, EDGE:, :] = spec[:, :, pl.ds(inner, near), :]
-    which = jnp.where(at == 0, 0, 1)
-
-    def add(w, f, c, total):
-        acc[smooth_slot(chan_count, w, f, c) - 2 * chan_count] = total
-
-    row_pass(lambda: row_band[which], lambda w, c: frame[w, c], rowwise, chan_count, 4)
-    column_pass(rowwise, matrix, smooth, add, chan_count)
+    inside = pl.multiple_of(jnp.where(at == 0, 0, n_rows - near), EDGE)
+    groups = []
+    if inner:
+        groups.append(rest(chan_count, turns) + (None,))
+    if rims:
+        for turn, first in enumerate(towards(chan_count, turns)):
+            groups.append((first, RIM, turn))
+
+    channels = []
+    for first, count, turn in groups:
+        base = len(channels)
+        channels += [first + i for i in range(count)]
+        for lane in range(0, n_cols, LANES):
+            cols = slice(lane, lane + LANES)
+            x = []
+            for i in range(count + 2 * RIM):
+                c = first - RIM + i
+                value = halo[jnp.clip(c, 0, chan_count - 1), :, cols].astype(f32)
+                if turn is not None and (i < RIM or i >= count + RIM):
+                    other = corners[turns - 1 - turn, i if i < RIM else i - count - RIM, :, cols]
+                    own = jnp.logical_and(c >= 0, c < chan_count)
+                    value = jnp.where(own, value, other.astype(f32))
+                x.append(value * wide(keep, RIM + c))
+            for i, both in means(x):
+                for w in range(2):
+                    frame[w, base + i, :EDGE, cols] = both[w]
+        for w in range(2):
+            frame[w, base : base + count, EDGE:, :] = spec[w, pl.ds(first, count), pl.ds(inside, near), :]
+
+    count = len(channels)
+    taps = row_band[jnp.where(at == 0, 0, 1)]
+    for w in range(2):
+        row_pass(taps, lambda i: frame[w, i], rowwise, list(range(count)), count, w * count)
+    if count < chan_count:
+        acc[...] = jnp.zeros_like(acc)
+
+    def put(f, slot, values):
+        w, c = slot // count, channels[slot % count]
+        start = pl.multiple_of((w * chan_count + c) * EDGE, EDGE)
+        target = smooth_slot(chan_count, w, f, c) - 2 * chan_count
+        put_tiles(smooth, squares, acc, f, start, target, values)
+
+    column_pass(rowwise, matrix, 2 * count, put)
     before = sums[: 2 * chan_count, :]
     total = sums[2 * chan_count :, :] + jnp.sum(acc[...], axis=1)
-    if pair == 0:
+    if peers:
+        sums_out[...] = share(jnp.concatenate([before, total]), sums_out)
+    else:
         sums_out[: 2 * chan_count, :] = before
         sums_out[2 * chan_count :, :] = total
-    else:
-        sums_out[...] = share(jnp.concatenate([before, total]), sums_out)
 
 
 def share(acc_sum, out):
@@ -282,13 +331,12 @@
             for part in parts:
                 for r in range(0, part.shape[0], 8):
                     for l in range(0, part.shape[1], LANES):
-                        value = part[r : r + 8, l : l + LANES]
-                        value = jnp.minimum(value * value, top)
+                        value = jnp.minimum(part[r : r + 8, l : l + LANES], top)
                         total = value if total is None else total + value
             acc[slot] = total
 
         for w in range(2):
-            clipped(spectral_slot(chan_count, w, c), [spec[w, c].astype(f32)])
+            clipped(spectral_slot(chan_count, w, c), [spec[w, c]])
             for f in range(2):
                 parts = []
                 for source in (middle, edge_one, edge_two):
@@ -303,13 +351,15 @@
 def ratio_kernel(pixels, keep, shared_in, spec, middle, edge_one, edge_two, out, scale, staged, sems):
     chan_count, n_rows, n_cols = out.shape
     scale[...] = 1.0 / jnp.sqrt(spread(shared_in) / pixels + epsilon)
+    for k in range(6):
+        rows = slice(k * chan_count, (k + 1) * chan_count)
+        scale[rows, :] = scale[rows, :] * keep[RIM : RIM + chan_count, :]
     parts = sems.shape[0]
     group = chan_count // parts
     tiles = [(middle, r, EDGE + r) for r in range(0, n_rows - 2 * EDGE, EDGE)]
     tiles += [(edge_one, 0, pair_rows(n_rows, 0)), (edge_two, 0, pair_rows(n_rows, 1))]
 
     def channel(c):
-        keep_tile = wide(keep, c)
         factors = [
             [wide(scale, spectral_slot(chan_count, w, c))]
             + [wide(scale, smooth_slot(chan_count, w, f, c)) for f in range(2)]
@@ -328,7 +378,7 @@
                     for value, factor in zip(values, factors[w]):
                         value = value * factor
                         best = value if best is None else jnp.maximum(best, value)
-                staged[c, rows, cols] = (best * keep_tile).astype(bf16)
+                staged[c, rows, cols] = best.astype(bf16)
 
     copies = []
     for p in range(parts):
@@ -344,13 +394,14 @@
     return [pl.BlockSpec(memory_space=s) for s in spaces]
 
 
-def call(kernel, ins, outs, scratch, flops, out_space=VMEM):
+def call(kernel, ins, outs, scratch, flops, out_space=VMEM, aliases={}):
     return pl.pallas_call(
         kernel,
         in_specs=specs(ins),
         out_specs=specs([out_space] * len(outs)),
         out_shape=[jax.ShapeDtypeStruct(s, d) for s, d in outs],
         scratch_shapes=scratch,
+        input_output_aliases=aliases,
         compiler_params=pltpu.CompilerParams(vmem_limit_bytes=32 * 2**20),
         cost_estimate=pl.CostEstimate(flops=flops, bytes_accessed=2**20, transcendentals=0),
     )
@@ -407,7 +458,7 @@
     rims, keep = call(
         rim_kernel,
         [HBM, HBM],
-        [((turns, RIM, n_rows, n_cols), bf16), ((chan_count + 8, LANES), f32)],
+        [((turns, RIM, n_rows, n_cols), bf16), ((chan_count + 2 * RIM, LANES), f32)],
         [
             SMEM((chan_count,), jnp.int32),
             VMEM((turns, RIM, n_rows, n_cols), bf16),
@@ -431,39 +482,51 @@
         return across(corners)
 
     corners_one = corners_of(first_pair)
-    corners_two = corners_of(second_pair)
-    spec, middle, sums = call(
+
+    mid_out = ((2, 2 * chan_count * mid, n_cols), f32)
+    sums_out = ((slots, LANES), f32)
+    spec, spec_squares, middle, middle_squares, sums = call(
         middle_kernel,
         [VMEM] * 5,
         [
             ((2, chan_count, n_rows, n_cols), bf16),
-            ((2, 2 * chan_count * mid, n_cols), f32),
-            ((slots, LANES), f32),
+            ((2, chan_count, n_rows, n_cols), f32),
+            mid_out,
+            mid_out,
+            sums_out,
         ],
-        [VMEM((2, 2 * chan_count * mid, n_cols), bf16), VMEM((slots, 8, LANES), f32)],
+        [VMEM(mid_out[0], bf16), VMEM((slots, 8, LANES), f32)],
         2 * 10**9,
     )(keep, own, rim, mid_band, matrix)
 
-    edge_out = ((2, 2 * chan_count * EDGE, n_cols), f32)
-    edge_scratch = [
-        VMEM((2, 2 * chan_count * EDGE, n_cols), bf16),
-        VMEM((slots - 2 * chan_count, 8, LANES), f32),
-        VMEM((2, chan_count, EDGE + near, n_cols), bf16),
-    ]
-    edge_one, sums = call(
-        functools.partial(edge_kernel, 0),
-        [VMEM] * 7,
-        [edge_out, ((slots, LANES), f32)],
-        edge_scratch,
-        10**9,
-    )(keep, first_pair, corners_one, spec, edge_band, matrix, sums)
-    edge_two, shared = call(
-        functools.partial(edge_kernel, 1),
-        [VMEM] * 7,
-        [edge_out, ((strips, width), f32)],
-        edge_scratch,
-        10**9,
-    )(keep, second_pair, corners_two, spec, edge_band, matrix, sums)
+    def edge(pair, inner, rims, last, *args):
+        count = (chan_count - turns * RIM) * inner + turns * RIM * rims
+        in_place = rims and not inner
+        out = ((2, 2 * chan_count * EDGE, n_cols), f32)
+        return call(
+            functools.partial(edge_kernel, pair, turns, inner, rims, last),
+            [VMEM] * len(args),
+            [out, out, ((strips, width), f32) if last else sums_out],
+            [
+                VMEM((2, 2 * count * EDGE, n_cols), bf16),
+                VMEM((slots - 2 * chan_count, 8, LANES), f32),
+                VMEM((2, count, EDGE + near, n_cols), bf16),
+            ],
+            10**9,
+            aliases={len(args) - 2: 0, len(args) - 1: 1} if in_place else {},
+        )(*args)
+
+    edge_one, one_squares, sums = edge(
+        0, True, True, False, keep, first_pair, corners_one, spec, edge_band, matrix, sums
+    )
+    corners_two = corners_of(second_pair)
+    edge_two, two_squares, sums = edge(
+        1, True, False, False, keep, second_pair, spec, edge_band, matrix, sums
+    )
+    edge_two, two_squares, shared = edge(
+        1, False, True, True, keep, second_pair, corners_two, spec, edge_band, matrix, sums,
+        edge_two, two_squares,
+    )
 
     shared = lax.all_to_all(shared, "strip", 0, 0, tiled=True)
     (shared,) = call(
@@ -472,7 +535,7 @@
         [((strips, width), f32)],
         [VMEM((width, LANES), f32), VMEM((slots, 8, LANES), f32)],
         10**8,
-    )(shared, spec, middle, edge_one, edge_two)
+    )(shared, spec_squares, middle_squares, one_squares, two_squares)
     shared = lax.all_to_all(shared, "strip", 0, 0, tiled=True)
     (out,) = call(
         functools.partial(ratio_kernel, pixels),

time: 47.5 us -> 46.2 us (0.973)
  Pallas kernels: 13.9 us -> 12.6 us
    pallas_call x2 -> x3, Pallas kernels: 3.34 us -> 2.55 us  [edge(): call(functools.partial(edge_kernel, pair, turns, inner, rims, last), [VME...]
  transfers between devices with their start and end apart: 5 -> 5, of which waited for: 1 -> 1; matrix products, arithmetic and copies ran while one was open for 0% -> 0% of each run, Pallas kernels for 15% -> 16%
where the time goes in v4:
time: 46.2 us; the launch traced here: 45.9 us
  blocking collectives  20.9 us (45%)
  Pallas kernels  12.6 us (27%)
  waiting for transfers between devices  7.96 us (17%)
  starting transfers between devices  4.4 us (10%)
    all_to_all x2, blocking collectives, shards(): shared = lax.all_to_all(shared, 'strip', 0, 0, tiled=True)  20.9 us
    ppermute x1, waiting for transfers between devices, shards(): first_pair = lax.ppermute(first_pair, 'strip', evens)  7.95 us
    ppermute x1, starting transfers between devices, shards(): first_pair = lax.ppermute(first_pair, 'strip', evens)  3.03 us
    pallas_call x1, Pallas kernels, shards(): call(middle_kernel, [VMEM] * 5, [((2, chan_count, n_rows, n_cols), bf16),...  2.92 us
    pallas_call x3, Pallas kernels, edge(): call(functools.partial(edge_kernel, pair, turns, inner, rims, last), [VME...  2.55 us
    pallas_call x1, Pallas kernels, shards(): call(functools.partial(ratio_kernel, pixels), [VMEM] * 6, [((chan_count,...  2.01 us
    pallas_call x1, Pallas kernels, shards(): call(functools.partial(clip_kernel, pixels), [VMEM] * 5, [((strips, width...  1.53 us
    pallas_call x1, Pallas kernels, shards(): call(load_kernel, [HBM] * 4, [(v.shape, bf16) for v in (sky_cube, mid_ban...  1.49 us
  transfers between devices with their start and end apart: 5, of which 1 were waited for; matrix products, arithmetic and copies ran while one was open for 0% of the time, Pallas kernels for 16%

profile of v4, /device:TPU:0, one launch (start us, length us, event | category | flops | bytes accessed | tf_op | source)
XLA Modules:
  0.0 45.9 jit_solution(18015915230609872265)
XLA Ops:
  0.0 1.0 %shard_map.56 = (bf16[16,16,512]{2,1,0:T(8,128)(2,1)S(1)}, bf16[16,16,512]{2,1,0:T(8,128)(2,1)S(1)}) custom-call(bf16[16,64,512]{2,1,0:T(8,128)(2,1)} %sky.5), custom_call_target="tpu_custom_call" | custom-call | flops 1000000 | bytes 1048576 | tf_op jit(solution)/shard_map/pallas_call | solution.py:440
  1.1 3.0 %collective-permute-start.3 = (bf16[16,16,512]{2,1,0:T(8,128)(2,1)S(1)}, bf16[16,16,512]{2,1,0:T(8,128)(2,1)S(1)}, u32[]{:S(2)}, u32[]{:S(2)}) collective-permute-start(bf16[16,16,512]{2,1,0:T(8,128)(2,1)S(1)} %get-tuple-element.35), channel_id=1, source_target_pairs={{0,2},{4,6},{8,10},{12,14},{2,0},{6,4},{10,8},{14,12},{1,3},{5,7},... | collective-permute-start | bytes 786440 | tf_op jit(solution)/shard_map/ppermute | solution.py:447
  4.1 1.0 %shard_map.55 = (bf16[1,3,64,512]{3,2,1,0:T(8,128)(2,1)S(1)}, f32[22,128]{1,0:T(8,128)S(1)}) custom-call(s32[16]{0:T(128)} %flags.1, bf16[16,64,512]{2,1,0:T(8,128)(2,1)} %sky.5), custom_call_target="tpu_custom_call" | custom-call | flops 1000000 | bytes 1048576 | tf_op jit(solution)/shard_map/pallas_call | solution.py:458
  5.1 0.1 collective-permute-start.2
  5.2 0.7 %collective-permute-start = (bf16[16,16,512]{2,1,0:T(8,128)(2,1)S(1)}, bf16[16,16,512]{2,1,0:T(8,128)(2,1)S(1)}, u32[]{:S(2)}, u32[]{:S(2)}) collective-permute-start(bf16[16,16,512]{2,1,0:T(8,128)(2,1)S(1)} %get-tuple-element.28), channel_id=1, source_target_pairs={{2,4},{6,8},{10,12},{4,2},{8,6},{12,10},{3,5},{7,9},{11,13},{5,3},... | collective-permute-start | bytes 786440 | tf_op jit(solution)/shard_map/ppermute | solution.py:448
  5.8 1.5 %shard_map.58 = (bf16[16,64,512]{2,1,0:T(8,128)(2,1)S(1)}, bf16[64,64]{1,0:T(8,128)(2,1)S(1)}, bf16[2,32,48]{2,1,0:T(8,128)(2,1)S(1)}, bf16[2,3,256,256]{3,2,1,0:T(8,128)(2,1)S(1)}) custom-call(bf16[16,64,512]{2,1,0:T(8,128)(2,1)} %sky.5, bf16[64,64]{1,0:T(8,128)(2,1)} %constant.9.mid_in, bf16[2,32,48]{2,1,0:T(8,128)(2,1)} %constant.10.edge_in, ...), custom_call_target="tpu_custom_call" | custom-call | flops 1000000 | bytes 1048576 | tf_op jit(solution)/shard_map/pallas_call | solution.py:470
  7.3 8.0 %collective-permute-done.3.halo.refs_1_ = bf16[16,16,512]{2,1,0:T(8,128)(2,1)S(1)} collective-permute-done((bf16[16,16,512]{2,1,0:T(8,128)(2,1)S(1)}, bf16[16,16,512]{2,1,0:T(8,128)(2,1)S(1)}, u32[]{:S(2)}, u32[]{:S(2)}) %collective-permute-start.3) | collective-permute-done | bytes 262176 | tf_op jit(solution)/shard_map/ppermute | solution.py:447
  15.3 0.1 collective-permute-start.4
  15.4 0.0 collective-permute-done.2.rim
  15.4 2.9 %shard_map.59 = (bf16[2,16,64,512]{3,2,1,0:T(8,128)(2,1)S(1)}, f32[2,16,64,512]{3,2,1,0:T(8,128)S(1)}, f32[2,1024,512]{2,1,0:T(8,128)S(1)}, f32[2,1024,512]{2,1,0:T(8,128)S(1)}, f32[96,128]{1,0:T(8,128)S(1)}) custom-call(f32[22,128]{1,0:T(8,128)S(1)} %get-tuple-element.27.keep.refs_0_, bf16[16,64,512]{2,1,0:T(8,128)(2,1)S(1)} %get-tuple-element.29.sky, ...), custom_call_target="tpu_custom_call" | custom-call | flops 2000000000 | bytes 1048576 | tf_op jit(solution)/shard_map/pallas_call | solution.py:488
  18.3 0.0 collective-permute-done.halo.refs_1_
  18.4 0.5 %collective-permute-start.1 = (bf16[1,3,16,512]{3,2,1,0:T(8,128)(2,1)S(1)}, bf16[1,3,16,512]{3,2,1,0:T(8,128)(2,1)S(1)}, u32[]{:S(2)}, u32[]{:S(2)}) collective-permute-start(bf16[1,3,16,512]{3,2,1,0:T(8,128)(2,1)S(1)} %shard_map.57), channel_id=1, source_target_pairs={{0,1},{1,0},{2,3},{3,2},{4,5},{5,4},{6,7},{7,6},{8,9},{9,8},{10,11... | collective-permute-start | bytes 147464 | tf_op jit(solution)/shard_map/ppermute | solution.py:455
  18.9 0.0 collective-permute-done.4.refs_2_
  18.9 1.1 %shard_map.61 = (f32[2,512,512]{2,1,0:T(8,128)S(1)}, f32[2,512,512]{2,1,0:T(8,128)S(1)}, f32[96,128]{1,0:T(8,128)S(1)}) custom-call(f32[22,128]{1,0:T(8,128)S(1)} %get-tuple-element.27.keep.refs_0_, bf16[16,16,512]{2,1,0:T(8,128)(2,1)S(1)} %collective-permute-done.3.halo.refs_1_, bf16[1,3,16,512]{3,2,1,0:T(8,128)(2,1)S(1)} %collective-permute-done.4.refs_2_, ...), custom_call_target="tpu_custom_call" | custom-call | flops 1000000000 | bytes 1048576 | tf_op jit(solution)/shard_map/pallas_call | solution.py:506
  20.0 1.0 %shard_map.62 = (f32[2,512,512]{2,1,0:T(8,128)S(1)}, f32[2,512,512]{2,1,0:T(8,128)S(1)}, f32[96,128]{1,0:T(8,128)S(1)}) custom-call(f32[22,128]{1,0:T(8,128)S(1)} %get-tuple-element.27.keep.refs_0_, bf16[16,16,512]{2,1,0:T(8,128)(2,1)S(1)} %collective-permute-done.halo.refs_1_, bf16[2,16,64,512]{3,2,1,0:T(8,128)(2,1)S(1)} %get-tuple-element.33.refs_3_.refs_2_.spec, ...), custom_call_target="tpu_custom_call" | custom-call | flops 1000000000 | bytes 1048576 | tf_op jit(solution)/shard_map/pallas_call | solution.py:506
  21.0 0.0 collective-permute-done.1.refs_2_
  21.0 0.5 %shard_map.63 = (f32[2,512,512]{2,1,0:T(8,128)S(1)}, f32[2,512,512]{2,1,0:T(8,128)S(1)}, f32[8,128]{1,0:T(8,128)S(1)}) custom-call(f32[22,128]{1,0:T(8,128)S(1)} %get-tuple-element.27.keep.refs_0_, bf16[16,16,512]{2,1,0:T(8,128)(2,1)S(1)} %collective-permute-done.halo.refs_1_, ...), custom_call_target="tpu_custom_call", output_to_operand_aliasing={{0}: (7, {}), {1}: (8, {})} | custom-call | flops 1000000000 | bytes 1048576 | tf_op jit(solution)/shard_map/pallas_call | solution.py:506
  21.5 12.0 %all_to_all.22 = f32[8,1,128]{2,1,0:T(1,128)S(1)} all-to-all(f32[8,1,128]{2,1,0:T(1,128)S(1)} %bitcast.11), channel_id=1, replica_groups=mesh['groups'=2,'strip'=8,'chan'=2] {'strip'}, dimensions={0} | all-to-all | bytes 8192 | tf_op jit(solution)/shard_map/all_to_all | solution.py:531
  33.5 1.5 %shard_map.64 = f32[8,128]{1,0:T(8,128)S(1)} custom-call(f32[8,128]{1,0:T(8,128)S(1)} %bitcast.9, f32[2,16,64,512]{3,2,1,0:T(8,128)S(1)} %get-tuple-element.42.spec, f32[2,1024,512]{2,1,0:T(8,128)S(1)} %get-tuple-element.43.middle, f32[2,512,512]{2,1,0:T(8,128)S(1)} %get-tuple-element.44.edge_one, f32[2,512,512]{2,1,0:T(8,128)S(1)} %get-tuple-element.45.edge_two), custom_call_target="tpu_custom_call" | custom-call | flops 100000000 | bytes 1048576 | tf_op jit(solution)/shard_map/pallas_call | solution.py:532
  35.1 8.9 %all_to_all.23 = f32[8,1,128]{2,1,0:T(1,128)S(1)} all-to-all(f32[8,1,128]{2,1,0:T(1,128)S(1)} %bitcast.10), channel_id=1, replica_groups=mesh['groups'=2,'strip'=8,'chan'=2] {'strip'}, dimensions={0} | all-to-all | bytes 8192 | tf_op jit(solution)/shard_map/all_to_all | solution.py:539
  43.9 2.0 %shard_map.65 = bf16[16,64,512]{2,1,0:T(8,128)(2,1)} custom-call(f32[22,128]{1,0:T(8,128)S(1)} %get-tuple-element.27.keep.refs_0_, f32[8,128]{1,0:T(8,128)S(1)} %bitcast.8, bf16[2,16,64,512]{3,2,1,0:T(8,128)(2,1)S(1)} %get-tuple-element.33.refs_3_.refs_2_.spec, f32[2,1024,512]{2,1,0:T(8,128)S(1)} %get-tuple-element.46.middle, ...), custom_call_target="tpu_custom_call" | custom-call | flops 100000000 | bytes 1048576 | tf_op jit(solution)/shard_map/pallas_call | solution.py:540
  (2 shorter events, 0.0 us)
Async XLA Ops:
  1.1 14.2 %collective-permute-start.3 = (bf16[16,16,512]{2,1,0:T(8,128)(2,1)S(1)}, bf16[16,16,512]{2,1,0:T(8,128)(2,1)S(1)}, u32[]{:S(2)}, u32[]{:S(2)}) collective-permute-start(bf16[16,16,512]{2,1,0:T(8,128)(2,1)S(1)} %get-tuple-element.35), channel_id=1, source_target_pairs={{0,2},{4,6},{8,10},{12,14},{2,0},{6,4},{10,8},{14,12},{1,3},{5,7},... | collective-permute-start | bytes 786440 | tf_op jit(solution)/shard_map/ppermute | solution.py:447
  5.1 10.3 %collective-permute-start.2 = (bf16[1,3,64,512]{3,2,1,0:T(8,128)(2,1)S(1)}, bf16[1,3,64,512]{3,2,1,0:T(8,128)(2,1)S(1)}, u32[]{:S(2)}, u32[]{:S(2)}) collective-permute-start(bf16[1,3,64,512]{3,2,1,0:T(8,128)(2,1)S(1)} %get-tuple-element.30), channel_id=1, source_target_pairs={{0,1},{1,0},{2,3},{3,2},{4,5},{5,4},{6,7},{7,6},{8,9},{9,8},{10,11... | collective-permute-start | bytes 589832 | tf_op jit(solution)/shard_map/ppermute | solution.py:455
  5.2 13.2 %collective-permute-start = (bf16[16,16,512]{2,1,0:T(8,128)(2,1)S(1)}, bf16[16,16,512]{2,1,0:T(8,128)(2,1)S(1)}, u32[]{:S(2)}, u32[]{:S(2)}) collective-permute-start(bf16[16,16,512]{2,1,0:T(8,128)(2,1)S(1)} %get-tuple-element.28), channel_id=1, source_target_pairs={{2,4},{6,8},{10,12},{4,2},{8,6},{12,10},{3,5},{7,9},{11,13},{5,3},... | collective-permute-start | bytes 786440 | tf_op jit(solution)/shard_map/ppermute | solution.py:448
  15.3 3.6 %collective-permute-start.4 = (bf16[1,3,16,512]{3,2,1,0:T(8,128)(2,1)S(1)}, bf16[1,3,16,512]{3,2,1,0:T(8,128)(2,1)S(1)}, u32[]{:S(2)}, u32[]{:S(2)}) collective-permute-start(bf16[1,3,16,512]{3,2,1,0:T(8,128)(2,1)S(1)} %shard_map.60), channel_id=1, source_target_pairs={{0,1},{1,0},{2,3},{3,2},{4,5},{5,4},{6,7},{7,6},{8,9},{9,8},{10,11... | collective-permute-start | bytes 147464 | tf_op jit(solution)/shard_map/ppermute | solution.py:455
  18.4 2.6 %collective-permute-start.1 = (bf16[1,3,16,512]{3,2,1,0:T(8,128)(2,1)S(1)}, bf16[1,3,16,512]{3,2,1,0:T(8,128)(2,1)S(1)}, u32[]{:S(2)}, u32[]{:S(2)}) collective-permute-start(bf16[1,3,16,512]{3,2,1,0:T(8,128)(2,1)S(1)} %shard_map.57), channel_id=1, source_target_pairs={{0,1},{1,0},{2,3},{3,2},{4,5},{5,4},{6,7},{7,6},{8,9},{9,8},{10,11... | collective-permute-start | bytes 147464 | tf_op jit(solution)/shard_map/ppermute | solution.py:455

commit v5 on v4

--- a/solution.py
+++ b/solution.py
@@ -124,7 +124,7 @@
             put(f, slot, values)
 
 
-def put_tiles(smooth, squares, acc, f, start, slot, values):
+def put_tiles(smooth, squares, acc, f, start, slot, values, add=False):
     rows = pl.ds(start, values[0].shape[0])
     total = None
     for i, value in enumerate(values):
@@ -134,7 +134,7 @@
         squares[f, rows, cols] = square
         part = fold(square)
         total = part if total is None else total + part
-    acc[slot] = total
+    acc[slot] = acc[slot] + total if add else total
 
 
 def run(copies):
@@ -187,14 +187,16 @@
     )
 
 
-def corner_kernel(keep, halo, corners):
-    chan_count, _, n_cols = halo.shape
+def corner_kernel(keep, first_pair, second_pair, corners):
+    chan_count, _, n_cols = first_pair.shape
     for turn, first in enumerate(towards(chan_count, corners.shape[0])):
-        for i in range(RIM):
-            factor = wide(keep, RIM + first + i)
-            for l in range(0, n_cols, LANES):
-                cols = slice(l, l + LANES)
-                corners[turn, i, :, cols] = (halo[first + i, :, cols].astype(f32) * factor).astype(bf16)
+        for pair, halo in enumerate((first_pair, second_pair)):
+            for i in range(RIM):
+                factor = wide(keep, RIM + first + i)
+                for l in range(0, n_cols, LANES):
+                    cols = slice(l, l + LANES)
+                    value = halo[first + i, :, cols].astype(f32) * factor
+                    corners[turn, pair * RIM + i, :, cols] = value.astype(bf16)
 
 
 def middle_kernel(keep, sky, rim, row_band, matrix, spec, spec_squares, smooth, squares, sums, rowwise, acc):
@@ -240,64 +242,75 @@
     sums[...] = jnp.sum(acc[...], axis=1)
 
 
-def edge_kernel(pair, turns, inner, rims, peers, *refs):
+def edge_kernel(pairs, turns, rims, *refs):
     refs = list(refs)
-    keep, halo = refs[:2]
-    del refs[:2]
-    corners = refs.pop(0) if rims else None
-    spec, row_band, matrix, sums = refs[:4]
-    if rims and not inner:
-        del refs[4:6]
-    smooth, squares, sums_out, rowwise, acc, frame = refs[-6:]
+
+    def take(count):
+        taken = refs[:count]
+        del refs[:count]
+        return taken
+
+    (keep,) = take(1)
+    halos = take(len(pairs))
+    corners = take(1)[0] if rims else None
+    spec, row_band, matrix, sums = take(4)
+    if rims:
+        take(2 * len(pairs))
+    outs = [take(2) for _ in pairs]
+    sums_out, rowwise, acc, frame = refs
     chan_count, n_rows, n_cols = spec.shape[1:]
     near = frame.shape[2] - EDGE
-    at = pair_rows(n_rows, pair)
-    inside = pl.multiple_of(jnp.where(at == 0, 0, n_rows - near), EDGE)
-    groups = []
-    if inner:
-        groups.append(rest(chan_count, turns) + (None,))
+    groups = [rest(chan_count, turns) + (None,)]
     if rims:
-        for turn, first in enumerate(towards(chan_count, turns)):
-            groups.append((first, RIM, turn))
-
-    channels = []
-    for first, count, turn in groups:
-        base = len(channels)
-        channels += [first + i for i in range(count)]
-        for lane in range(0, n_cols, LANES):
-            cols = slice(lane, lane + LANES)
-            x = []
-            for i in range(count + 2 * RIM):
-                c = first - RIM + i
-                value = halo[jnp.clip(c, 0, chan_count - 1), :, cols].astype(f32)
-                if turn is not None and (i < RIM or i >= count + RIM):
-                    other = corners[turns - 1 - turn, i if i < RIM else i - count - RIM, :, cols]
-                    own = jnp.logical_and(c >= 0, c < chan_count)
-                    value = jnp.where(own, value, other.astype(f32))
-                x.append(value * wide(keep, RIM + c))
-            for i, both in means(x):
-                for w in range(2):
-                    frame[w, base + i, :EDGE, cols] = both[w]
-        for w in range(2):
-            frame[w, base : base + count, EDGE:, :] = spec[w, pl.ds(first, count), pl.ds(inside, near), :]
-
-    count = len(channels)
-    taps = row_band[jnp.where(at == 0, 0, 1)]
+        groups = [(first, RIM, turn) for turn, first in enumerate(towards(chan_count, turns))]
+
+    planes, taps = [], []
+    for side, pair in enumerate(pairs):
+        at = pair_rows(n_rows, pair)
+        inside = pl.multiple_of(jnp.where(at == 0, 0, n_rows - near), EDGE)
+        taps.append(row_band[jnp.where(at == 0, 0, 1)])
+        halo = halos[side]
+        for first, count, turn in groups:
+            base = len(planes)
+            planes += [(side, first + i) for i in range(count)]
+            for lane in range(0, n_cols, LANES):
+                cols = slice(lane, lane + LANES)
+                x = []
+                for i in range(count + 2 * RIM):
+                    c = first - RIM + i
+                    value = halo[jnp.clip(c, 0, chan_count - 1), :, cols].astype(f32)
+                    if turn is not None and (i < RIM or i >= count + RIM):
+                        at_rim = pair * RIM + (i if i < RIM else i - count - RIM)
+                        other = corners[turns - 1 - turn, at_rim, :, cols]
+                        own = jnp.logical_and(c >= 0, c < chan_count)
+                        value = jnp.where(own, value, other.astype(f32))
+                    x.append(value * wide(keep, RIM + c))
+                for i, both in means(x):
+                    for w in range(2):
+                        frame[w, base + i, :EDGE, cols] = both[w]
+            for w in range(2):
+                inner = spec[w, pl.ds(first, count), pl.ds(inside, near), :]
+                frame[w, base : base + count, EDGE:, :] = inner
+
+    count = len(planes)
+    each = count // len(pairs)
     for w in range(2):
-        row_pass(taps, lambda i: frame[w, i], rowwise, list(range(count)), count, w * count)
-    if count < chan_count:
-        acc[...] = jnp.zeros_like(acc)
+        for side in range(len(pairs)):
+            slots = list(range(side * each, (side + 1) * each))
+            row_pass(taps[side], lambda i: frame[w, i], rowwise, slots, each, w * count + side * each)
+    acc[...] = jnp.zeros_like(acc)
 
     def put(f, slot, values):
-        w, c = slot // count, channels[slot % count]
+        w = slot // count
+        side, c = planes[slot % count]
         start = pl.multiple_of((w * chan_count + c) * EDGE, EDGE)
         target = smooth_slot(chan_count, w, f, c) - 2 * chan_count
-        put_tiles(smooth, squares, acc, f, start, target, values)
+        put_tiles(*outs[side], acc, f, start, target, values, side > 0)
 
     column_pass(rowwise, matrix, 2 * count, put)
     before = sums[: 2 * chan_count, :]
     total = sums[2 * chan_count :, :] + jnp.sum(acc[...], axis=1)
-    if peers:
+    if rims:
         sums_out[...] = share(jnp.concatenate([before, total]), sums_out)
     else:
         sums_out[: 2 * chan_count, :] = before
@@ -402,7 +415,7 @@
         out_shape=[jax.ShapeDtypeStruct(s, d) for s, d in outs],
         scratch_shapes=scratch,
         input_output_aliases=aliases,
-        compiler_params=pltpu.CompilerParams(vmem_limit_bytes=32 * 2**20),
+        compiler_params=pltpu.CompilerParams(vmem_limit_bytes=12 * 2**20),
         cost_estimate=pl.CostEstimate(flops=flops, bytes_accessed=2**20, transcendentals=0),
     )
 
@@ -475,14 +488,6 @@
         10**6,
     )(sky_cube, mid_band, edge_band, matrix)
 
-    def corners_of(halo):
-        (corners,) = call(
-            corner_kernel, [VMEM] * 2, [((turns, RIM, EDGE, n_cols), bf16)], [], 10**6
-        )(keep, halo)
-        return across(corners)
-
-    corners_one = corners_of(first_pair)
-
     mid_out = ((2, 2 * chan_count * mid, n_cols), f32)
     sums_out = ((slots, LANES), f32)
     spec, spec_squares, middle, middle_squares, sums = call(
@@ -499,34 +504,34 @@
         2 * 10**9,
     )(keep, own, rim, mid_band, matrix)
 
-    def edge(pair, inner, rims, last, *args):
-        count = (chan_count - turns * RIM) * inner + turns * RIM * rims
-        in_place = rims and not inner
-        out = ((2, 2 * chan_count * EDGE, n_cols), f32)
+    (corners,) = call(
+        corner_kernel, [VMEM] * 3, [((turns, 2 * RIM, EDGE, n_cols), bf16)], [], 10**6
+    )(keep, first_pair, second_pair)
+    corners = across(corners)
+
+    def edge(pairs, rims, *args):
+        count = turns * RIM if rims else chan_count - turns * RIM
+        count *= len(pairs)
+        outs = [((2, 2 * chan_count * EDGE, n_cols), f32)] * (2 * len(pairs))
+        in_place = {len(args) - len(outs) + i: i for i in range(len(outs))}
         return call(
-            functools.partial(edge_kernel, pair, turns, inner, rims, last),
+            functools.partial(edge_kernel, pairs, turns, rims),
             [VMEM] * len(args),
-            [out, out, ((strips, width), f32) if last else sums_out],
+            outs + [((strips, width), f32) if rims else sums_out],
             [
                 VMEM((2, 2 * count * EDGE, n_cols), bf16),
                 VMEM((slots - 2 * chan_count, 8, LANES), f32),
                 VMEM((2, count, EDGE + near, n_cols), bf16),
             ],
             10**9,
-            aliases={len(args) - 2: 0, len(args) - 1: 1} if in_place else {},
+            aliases=in_place if rims else {},
         )(*args)
 
-    edge_one, one_squares, sums = edge(
-        0, True, True, False, keep, first_pair, corners_one, spec, edge_band, matrix, sums
-    )
-    corners_two = corners_of(second_pair)
-    edge_two, two_squares, sums = edge(
-        1, True, False, False, keep, second_pair, spec, edge_band, matrix, sums
-    )
-    edge_two, two_squares, shared = edge(
-        1, False, True, True, keep, second_pair, corners_two, spec, edge_band, matrix, sums,
-        edge_two, two_squares,
-    )
+    shared_args = (spec, edge_band, matrix)
+    *two, sums = edge((1,), False, keep, second_pair, *shared_args, sums)
+    *one, sums = edge((0,), False, keep, first_pair, *shared_args, sums)
+    args = (keep, first_pair, second_pair, corners, *shared_args, sums)
+    edge_one, one_squares, edge_two, two_squares, shared = edge((0, 1), True, *args, *one, *two)
 
     shared = lax.all_to_all(shared, "strip", 0, 0, tiled=True)
     (shared,) = call(

time: 46.2 us -> 44.6 us (0.965)
  waiting for transfers between devices: 7.96 us -> 6.72 us
  starting transfers between devices: 4.4 us -> 3.86 us
    ppermute x1, waiting for transfers between devices: 7.95 us -> 6.71 us  [shards(): first_pair = lax.ppermute(first_pair, 'strip', evens)]
    ppermute x1, starting transfers between devices: 3.03 us -> 2.57 us  [shards(): first_pair = lax.ppermute(first_pair, 'strip', evens)]
    pallas_call x5 -> x4, Pallas kernels: 2.59 us -> 2.63 us  [the longest x3 2.61 us: edge(): call(functools.partial(edge_kernel, pairs, turns, rims), [VMEM] * len(arg...]
  transfers between devices with their start and end apart: 5 -> 4, of which waited for: 1 -> 1; matrix products, arithmetic and copies ran while one was open for 0% -> 0% of each run, Pallas kernels for 16% -> 17%
where the time goes in v5:
time: 44.6 us; the launch traced here: 44.4 us
  blocking collectives  21 us (47%)
  Pallas kernels  12.7 us (28%)
  waiting for transfers between devices  6.72 us (15%)
  starting transfers between devices  3.86 us (9%)
    all_to_all x2, blocking collectives, shards(): shared = lax.all_to_all(shared, 'strip', 0, 0, tiled=True)  21 us
    ppermute x1, waiting for transfers between devices, shards(): first_pair = lax.ppermute(first_pair, 'strip', evens)  6.71 us
    pallas_call x1, Pallas kernels, shards(): call(middle_kernel, [VMEM] * 5, [((2, chan_count, n_rows, n_cols), bf16),...  2.93 us
    pallas_call x3, Pallas kernels, edge(): call(functools.partial(edge_kernel, pairs, turns, rims), [VMEM] * len(arg...  2.61 us
    ppermute x1, starting transfers between devices, shards(): first_pair = lax.ppermute(first_pair, 'strip', evens)  2.57 us
    pallas_call x1, Pallas kernels, shards(): call(functools.partial(ratio_kernel, pixels), [VMEM] * 6, [((chan_count,...  2.01 us
    pallas_call x1, Pallas kernels, shards(): call(functools.partial(clip_kernel, pixels), [VMEM] * 5, [((strips, width...  1.6 us
    pallas_call x1, Pallas kernels, shards(): call(load_kernel, [HBM] * 4, [(v.shape, bf16) for v in (sky_cube, mid_ban...  1.49 us
  transfers between devices with their start and end apart: 4, of which 1 were waited for; matrix products, arithmetic and copies ran while one was open for 0% of the time, Pallas kernels for 17%

profile of v5, /device:TPU:0, one launch (start us, length us, event | category | flops | bytes accessed | tf_op | source)
XLA Modules:
  0.0 44.4 jit_solution(15564013617629109820)
XLA Ops:
  0.0 1.0 %shard_map.55 = (bf16[1,3,64,512]{3,2,1,0:T(8,128)(2,1)S(1)}, f32[22,128]{1,0:T(8,128)S(1)}) custom-call(s32[16]{0:T(128)} %flags.1, bf16[16,64,512]{2,1,0:T(8,128)(2,1)} %sky.5), custom_call_target="tpu_custom_call" | custom-call | flops 1000000 | bytes 1048576 | tf_op jit(solution)/shard_map/pallas_call | solution.py:471
  1.0 0.6 %collective-permute-start.3 = (bf16[1,3,64,512]{3,2,1,0:T(8,128)(2,1)S(1)}, bf16[1,3,64,512]{3,2,1,0:T(8,128)(2,1)S(1)}, u32[]{:S(2)}, u32[]{:S(2)}) collective-permute-start(bf16[1,3,64,512]{3,2,1,0:T(8,128)(2,1)S(1)} %get-tuple-element.33), channel_id=1, source_target_pairs={{0,1},{1,0},{2,3},{3,2},{4,5},{5,4},{6,7},{7,6},{8,9},{9,8},{10,11... | collective-permute-start | bytes 589832 | tf_op jit(solution)/shard_map/ppermute | solution.py:468
  1.6 1.0 %shard_map.56 = (bf16[16,16,512]{2,1,0:T(8,128)(2,1)S(1)}, bf16[16,16,512]{2,1,0:T(8,128)(2,1)S(1)}) custom-call(bf16[16,64,512]{2,1,0:T(8,128)(2,1)} %sky.5), custom_call_target="tpu_custom_call" | custom-call | flops 1000000 | bytes 1048576 | tf_op jit(solution)/shard_map/pallas_call | solution.py:453
  2.6 2.6 %collective-permute-start = (bf16[16,16,512]{2,1,0:T(8,128)(2,1)S(1)}, bf16[16,16,512]{2,1,0:T(8,128)(2,1)S(1)}, u32[]{:S(2)}, u32[]{:S(2)}) collective-permute-start(bf16[16,16,512]{2,1,0:T(8,128)(2,1)S(1)} %get-tuple-element.30), channel_id=1, source_target_pairs={{0,2},{4,6},{8,10},{12,14},{2,0},{6,4},{10,8},{14,12},{1,3},{5,7},... | collective-permute-start | bytes 786440 | tf_op jit(solution)/shard_map/ppermute | solution.py:460
  5.2 0.7 %collective-permute-start.1 = (bf16[16,16,512]{2,1,0:T(8,128)(2,1)S(1)}, bf16[16,16,512]{2,1,0:T(8,128)(2,1)S(1)}, u32[]{:S(2)}, u32[]{:S(2)}) collective-permute-start(bf16[16,16,512]{2,1,0:T(8,128)(2,1)S(1)} %get-tuple-element.31), channel_id=1, source_target_pairs={{2,4},{6,8},{10,12},{4,2},{8,6},{12,10},{3,5},{7,9},{11,13},{5,3},... | collective-permute-start | bytes 786440 | tf_op jit(solution)/shard_map/ppermute | solution.py:461
  5.9 1.5 %shard_map.58 = (bf16[16,64,512]{2,1,0:T(8,128)(2,1)S(1)}, bf16[64,64]{1,0:T(8,128)(2,1)S(1)}, bf16[2,32,48]{2,1,0:T(8,128)(2,1)S(1)}, bf16[2,3,256,256]{3,2,1,0:T(8,128)(2,1)S(1)}) custom-call(bf16[16,64,512]{2,1,0:T(8,128)(2,1)} %sky.5, bf16[64,64]{1,0:T(8,128)(2,1)} %constant.9.mid_in, bf16[2,32,48]{2,1,0:T(8,128)(2,1)} %constant.10.edge_in, ...), custom_call_target="tpu_custom_call" | custom-call | flops 1000000 | bytes 1048576 | tf_op jit(solution)/shard_map/pallas_call | solution.py:483
  7.4 0.0 collective-permute-done.3.rim
  7.4 2.9 %shard_map.59 = (bf16[2,16,64,512]{3,2,1,0:T(8,128)(2,1)S(1)}, f32[2,16,64,512]{3,2,1,0:T(8,128)S(1)}, f32[2,1024,512]{2,1,0:T(8,128)S(1)}, f32[2,1024,512]{2,1,0:T(8,128)S(1)}, f32[96,128]{1,0:T(8,128)S(1)}) custom-call(f32[22,128]{1,0:T(8,128)S(1)} %get-tuple-element.29.keep.refs_0_, bf16[16,64,512]{2,1,0:T(8,128)(2,1)S(1)} %get-tuple-element.32.sky, ...), custom_call_target="tpu_custom_call" | custom-call | flops 2000000000 | bytes 1048576 | tf_op jit(solution)/shard_map/pallas_call | solution.py:493
  10.3 6.7 %collective-permute-done.first_pair.refs_1_ = bf16[16,16,512]{2,1,0:T(8,128)(2,1)S(1)} collective-permute-done((bf16[16,16,512]{2,1,0:T(8,128)(2,1)S(1)}, bf16[16,16,512]{2,1,0:T(8,128)(2,1)S(1)}, u32[]{:S(2)}, u32[]{:S(2)}) %collective-permute-start) | collective-permute-done | bytes 262176 | tf_op jit(solution)/shard_map/ppermute | solution.py:460
  17.0 0.0 collective-permute-done.1.second_pair.refs_1_.refs_2_
  17.0 0.1 collective-permute-start.2
  17.1 1.0 %shard_map.60 = (f32[2,512,512]{2,1,0:T(8,128)S(1)}, f32[2,512,512]{2,1,0:T(8,128)S(1)}, f32[96,128]{1,0:T(8,128)S(1)}) custom-call(f32[22,128]{1,0:T(8,128)S(1)} %get-tuple-element.29.keep.refs_0_, bf16[16,16,512]{2,1,0:T(8,128)(2,1)S(1)} %collective-permute-done.1.second_pair.refs_1_.refs_2_, ...), custom_call_target="tpu_custom_call" | custom-call | flops 1000000000 | bytes 1048576 | tf_op jit(solution)/shard_map/pallas_call | solution.py:517
  18.1 1.0 %shard_map.61 = (f32[2,512,512]{2,1,0:T(8,128)S(1)}, f32[2,512,512]{2,1,0:T(8,128)S(1)}, f32[96,128]{1,0:T(8,128)S(1)}) custom-call(f32[22,128]{1,0:T(8,128)S(1)} %get-tuple-element.29.keep.refs_0_, bf16[16,16,512]{2,1,0:T(8,128)(2,1)S(1)} %collective-permute-done.first_pair.refs_1_, bf16[2,16,64,512]{3,2,1,0:T(8,128)(2,1)S(1)} %get-tuple-element.36.refs_2_.refs_4_.spec, ...), custom_call_target="tpu_custom_call" | custom-call | flops 1000000000 | bytes 1048576 | tf_op jit(solution)/shard_map/pallas_call | solution.py:517
  19.0 0.0 collective-permute-done.2.refs_3_
  19.0 0.7 %shard_map.62 = (f32[2,512,512]{2,1,0:T(8,128)S(1)}, f32[2,512,512]{2,1,0:T(8,128)S(1)}, f32[2,512,512]{2,1,0:T(8,128)S(1)}, f32[2,512,512]{2,1,0:T(8,128)S(1)}, f32[8,128]{1,0:T(8,128)S(1)}) custom-call(f32[22,128]{1,0:T(8,128)S(1)} %get-tuple-element.29.keep.refs_0_, ...), custom_call_target="tpu_custom_call", output_to_operand_aliasing={{0}: (8, {}), {1}: (9, {}), {2}: (10, {}), {3}: (11, {})} | custom-call | flops 1000000000 | bytes 1048576 | tf_op jit(solution)/shard_map/pallas_call | solution.py:517
  19.7 12.2 %all_to_all.22 = f32[8,1,128]{2,1,0:T(1,128)S(1)} all-to-all(f32[8,1,128]{2,1,0:T(1,128)S(1)} %bitcast.11), channel_id=1, replica_groups=mesh['groups'=2,'strip'=8,'chan'=2] {'strip'}, dimensions={0} | all-to-all | bytes 8192 | tf_op jit(solution)/shard_map/all_to_all | solution.py:536
  31.9 1.6 %shard_map.63 = f32[8,128]{1,0:T(8,128)S(1)} custom-call(f32[8,128]{1,0:T(8,128)S(1)} %bitcast.9, f32[2,16,64,512]{3,2,1,0:T(8,128)S(1)} %get-tuple-element.46.spec, f32[2,1024,512]{2,1,0:T(8,128)S(1)} %get-tuple-element.47.middle, f32[2,512,512]{2,1,0:T(8,128)S(1)} %get-tuple-element.48.edge_one, f32[2,512,512]{2,1,0:T(8,128)S(1)} %get-tuple-element.49.edge_two), custom_call_target="tpu_custom_call" | custom-call | flops 100000000 | bytes 1048576 | tf_op jit(solution)/shard_map/pallas_call | solution.py:537
  33.5 8.9 %all_to_all.23 = f32[8,1,128]{2,1,0:T(1,128)S(1)} all-to-all(f32[8,1,128]{2,1,0:T(1,128)S(1)} %bitcast.10), channel_id=1, replica_groups=mesh['groups'=2,'strip'=8,'chan'=2] {'strip'}, dimensions={0} | all-to-all | bytes 8192 | tf_op jit(solution)/shard_map/all_to_all | solution.py:544
  42.4 2.0 %shard_map.64 = bf16[16,64,512]{2,1,0:T(8,128)(2,1)} custom-call(f32[22,128]{1,0:T(8,128)S(1)} %get-tuple-element.29.keep.refs_0_, f32[8,128]{1,0:T(8,128)S(1)} %bitcast.8, bf16[2,16,64,512]{3,2,1,0:T(8,128)(2,1)S(1)} %get-tuple-element.36.refs_2_.refs_4_.spec, f32[2,1024,512]{2,1,0:T(8,128)S(1)} %get-tuple-element.50.middle, ...), custom_call_target="tpu_custom_call" | custom-call | flops 100000000 | bytes 1048576 | tf_op jit(solution)/shard_map/pallas_call | solution.py:545
  (1 shorter events, 0.0 us)
Async XLA Ops:
  1.0 6.4 %collective-permute-start.3 = (bf16[1,3,64,512]{3,2,1,0:T(8,128)(2,1)S(1)}, bf16[1,3,64,512]{3,2,1,0:T(8,128)(2,1)S(1)}, u32[]{:S(2)}, u32[]{:S(2)}) collective-permute-start(bf16[1,3,64,512]{3,2,1,0:T(8,128)(2,1)S(1)} %get-tuple-element.33), channel_id=1, source_target_pairs={{0,1},{1,0},{2,3},{3,2},{4,5},{5,4},{6,7},{7,6},{8,9},{9,8},{10,11... | collective-permute-start | bytes 589832 | tf_op jit(solution)/shard_map/ppermute | solution.py:468
  2.6 14.4 %collective-permute-start = (bf16[16,16,512]{2,1,0:T(8,128)(2,1)S(1)}, bf16[16,16,512]{2,1,0:T(8,128)(2,1)S(1)}, u32[]{:S(2)}, u32[]{:S(2)}) collective-permute-start(bf16[16,16,512]{2,1,0:T(8,128)(2,1)S(1)} %get-tuple-element.30), channel_id=1, source_target_pairs={{0,2},{4,6},{8,10},{12,14},{2,0},{6,4},{10,8},{14,12},{1,3},{5,7},... | collective-permute-start | bytes 786440 | tf_op jit(solution)/shard_map/ppermute | solution.py:460
  5.2 11.8 %collective-permute-start.1 = (bf16[16,16,512]{2,1,0:T(8,128)(2,1)S(1)}, bf16[16,16,512]{2,1,0:T(8,128)(2,1)S(1)}, u32[]{:S(2)}, u32[]{:S(2)}) collective-permute-start(bf16[16,16,512]{2,1,0:T(8,128)(2,1)S(1)} %get-tuple-element.31), channel_id=1, source_target_pairs={{2,4},{6,8},{10,12},{4,2},{8,6},{12,10},{3,5},{7,9},{11,13},{5,3},... | collective-permute-start | bytes 786440 | tf_op jit(solution)/shard_map/ppermute | solution.py:461
  17.0 2.0 %collective-permute-start.2 = (bf16[1,6,16,512]{3,2,1,0:T(8,128)(2,1)S(1)}, bf16[1,6,16,512]{3,2,1,0:T(8,128)(2,1)S(1)}, u32[]{:S(2)}, u32[]{:S(2)}) collective-permute-start(bf16[1,6,16,512]{3,2,1,0:T(8,128)(2,1)S(1)} %shard_map.57), channel_id=1, source_target_pairs={{0,1},{1,0},{2,3},{3,2},{4,5},{5,4},{6,7},{7,6},{8,9},{9,8},{10,11... | collective-permute-start | bytes 294920 | tf_op jit(solution)/shard_map/ppermute | solution.py:468
